TPU v7x, 512 devices: a whole 4x8x8 slice. The times are simulated.
512 devices in a mesh: skill: 64 (over y_lo, x, z), tensor: 8 (over y_hi, core).
Axes of the slice: x: 4, y: 8 (y_hi: 4, y_lo: 2; y = y_hi * 2 + y_lo), z: 8, core: 2. Of those that a mesh axis runs over, the one named last changes fastest.
Arguments:
- stored_inputs: bfloat16 [64, 256, 8192], P('skill', None, 'tensor'), may hold values from -6 to 6
- stored_output_gradient: bfloat16 [64, 256, 15360], P('skill', None, 'tensor'), may hold values from -6 to 6
- training_token_index: int32 [64, 256], P('skill'), may hold values from 0 to 255
- validation_inputs: bfloat16 [64, 512, 8192], P('skill', None, 'tensor'), may hold values from -6 to 6
- validation_output_gradient: bfloat16 [64, 512, 15360], P('skill', None, 'tensor'), may hold values from -6 to 6
- validation_row_skill: int32 [64, 512], P('skill'), may hold values from 0 to 63
- adapter_down_init: bfloat16 [64, 8192, 64], P('skill', 'tensor'), may hold values from -0.0625 to 0.0625
Outputs:
- own_delta: float32 [64, 17], P('skill')
- other_delta: float32 [64, 17], P('skill')
All inputs are finite; a program needn't handle non-finite values.
Results may differ from a plain program's by a relative error of at most 0.0042.
Values may be sent and summed in bfloat16 or wider, within the bound.
A program may use at most 64 MiB of HBM per device.

v0:
```python
import jax
import jax.numpy as jnp
from jax import lax
from jax.sharding import PartitionSpec as P


def from_behind(block, axis, distance):
    devices = range(lax.axis_size(axis))
    route = [((i - distance) % len(devices), i) for i in devices]
    return lax.ppermute(block, axis, route)


def evaluate(down_piece, up_piece, valid_act, valid_cot, own_mask, other_mask):
    partial_value = jnp.dot(valid_act, down_piece, preferred_element_type=jnp.float32)
    summed = lax.psum(partial_value, "tensor")
    cot_proj = lax.dot_general(
        valid_cot, up_piece, (((1,), (1,)), ((), ())), preferred_element_type=jnp.float32
    )
    row_change = jnp.sum(summed * cot_proj, axis=1)
    return jnp.stack([jnp.sum(row_change * own_mask), jnp.sum(row_change * other_mask)])


def on_device(
    stored_inputs,
    stored_output_gradient,
    training_token_index,
    validation_inputs,
    validation_output_gradient,
    validation_row_skill,
    adapter_down_init,
):
    chosen = training_token_index[0]
    train_act = jnp.take(stored_inputs[0], chosen, axis=0)
    train_cot = jnp.take(stored_output_gradient[0], chosen, axis=0)
    local_down_factor = adapter_down_init[0]
    partial_value = jnp.dot(train_act, local_down_factor, preferred_element_type=jnp.float32)
    proj = lax.psum(partial_value, "tensor").astype(jnp.bfloat16)
    product = lax.dot_general(
        proj, train_cot, (((0,), (0,)), ((), ())), preferred_element_type=jnp.float32
    )
    up_local = (product * (-1.0 / chosen.shape[0])).astype(jnp.bfloat16)
    valid_act = validation_inputs[0]
    valid_cot = validation_output_gradient[0]
    labels = validation_row_skill[0]
    my_skill = lax.axis_index("skill")
    own_mask = (labels == my_skill).astype(jnp.float32)
    other_mask = 1.0 - own_mask

    def score(down_piece, up_piece):
        return evaluate(down_piece, up_piece, valid_act, valid_cot, own_mask, other_mask)

    reach_count = lax.axis_size("skill") // 8
    column_count = 2 * reach_count + 1
    scores = jnp.zeros((column_count, 2), jnp.float32)
    first_down, first_up = from_behind((local_down_factor, up_local), "skill", reach_count)

    def advance(column, carry):
        held_down, held_up, table = carry
        table = table.at[column].set(score(held_down, held_up))
        held_down, held_up = from_behind((held_down, held_up), "skill", -1)
        return (held_down, held_up, table)

    last_down, last_up, scores = lax.fori_loop(
        0, column_count - 1, advance, (first_down, first_up, scores)
    )
    scores = scores.at[column_count - 1].set(score(last_down, last_up))
    totals = lax.psum(scores, "tensor")
    own_count = jnp.maximum(jnp.sum(own_mask), 1.0)
    other_count = jnp.maximum(jnp.sum(other_mask), 1.0)
    own_delta = (totals[:, 0] / own_count)[None, :]
    other_delta = (totals[:, 1] / other_count)[None, :]
    return (own_delta, other_delta)


def solution(mesh):
    in_specs = (
        P("skill", None, "tensor"),
        P("skill", None, "tensor"),
        P("skill", None),
        P("skill", None, "tensor"),
        P("skill", None, "tensor"),
        P("skill", None),
        P("skill", "tensor", None),
    )
    out_specs = (P("skill", None), P("skill", None))
    return jax.shard_map(
        on_device, mesh=mesh, in_specs=in_specs, out_specs=out_specs, check_vma=False
    )
```

profile of v0, /device:TPU:7, one launch (start us, length us, event | category | flops | bytes accessed | tf_op | source)
XLA Modules:
  0.0 1525.1 jit_solution(34875046202805492)
XLA Ops:
  12.5 28.2 %psum.32 = bf16[256,64]{1,0:T(8,128)(2,1)S(1)} all-reduce(f32[256,64]{1,0:T(8,128)S(1)} %fusion.4), channel_id=1, replica_groups=mesh['skill'=64,'tensor'=8] {'tensor'}, use_global_device_ids=true, to_apply=%region_0.1 | all-reduce | flops 16384 | bytes 98304 | tf_op jit(solution)/shard_map/psum | solution.py:37
  47.7 3.3 collective-permute-start.2
  51.1 5.0 collective-permute-done.2
  56.1 1351.9 %while.19 = (s32[]{:T(128)}, bf16[1024,64]{1,0:T(8,128)(2,1)}, bf16[64,1920]{1,0:T(8,128)(2,1)}, f32[17,2]{1,0:T(8,128)S(1)}, bf16[512,1024]{1,0:T(8,128)(2,1)},...) while((s32[]{:T(128)}, bf16[1024,64]{1,0:T(8,128)(2,1)}, ...), condition=%wide.region_7.8_spmd, body=%wide.region_1.7_spmd.sunk | while | flops 193037824 | bytes 6709567 | solution.py:63
  59.5 11.3 collective-permute-start
  74.6 70.0 %all-reduce.5.cloned.1.call-done = f32[512,64]{0,1:T(8,128)} async-done(((f32[512,64]{0,1:T(8,128)}), f32[512,64]{0,1:T(8,128)}) %all-reduce.5.cloned.1.call-update) | async-done | bytes 131088 | tf_op jit(solution)/shard_map/while/body/eval_jaxpr/psum | solution.py:15
  152.2 5.9 collective-permute-start
  159.0 2.9 collective-permute-start.1
  162.6 66.1 %all-reduce.5.cloned.1.call-done = f32[512,64]{0,1:T(8,128)} async-done(((f32[512,64]{0,1:T(8,128)}), f32[512,64]{0,1:T(8,128)}) %all-reduce.5.cloned.1.call-update) | async-done | bytes 131088 | tf_op jit(solution)/shard_map/while/body/eval_jaxpr/psum | solution.py:15
  236.4 5.9 collective-permute-start
  243.2 2.9 collective-permute-start.1
  246.8 66.1 %all-reduce.5.cloned.1.call-done = f32[512,64]{0,1:T(8,128)} async-done(((f32[512,64]{0,1:T(8,128)}), f32[512,64]{0,1:T(8,128)}) %all-reduce.5.cloned.1.call-update) | async-done | bytes 131088 | tf_op jit(solution)/shard_map/while/body/eval_jaxpr/psum | solution.py:15
  320.6 5.9 collective-permute-start
  327.4 2.9 collective-permute-start.1
  331.0 65.7 %all-reduce.5.cloned.1.call-done = f32[512,64]{0,1:T(8,128)} async-done(((f32[512,64]{0,1:T(8,128)}), f32[512,64]{0,1:T(8,128)}) %all-reduce.5.cloned.1.call-update) | async-done | bytes 131088 | tf_op jit(solution)/shard_map/while/body/eval_jaxpr/psum | solution.py:15
  404.3 5.9 collective-permute-start
  411.2 2.9 collective-permute-start.1
  414.7 65.7 %all-reduce.5.cloned.1.call-done = f32[512,64]{0,1:T(8,128)} async-done(((f32[512,64]{0,1:T(8,128)}), f32[512,64]{0,1:T(8,128)}) %all-reduce.5.cloned.1.call-update) | async-done | bytes 131088 | tf_op jit(solution)/shard_map/while/body/eval_jaxpr/psum | solution.py:15
  488.1 5.9 collective-permute-start
  498.5 65.7 %all-reduce.5.cloned.1.call-done = f32[512,64]{0,1:T(8,128)} async-done(((f32[512,64]{0,1:T(8,128)}), f32[512,64]{0,1:T(8,128)}) %all-reduce.5.cloned.1.call-update) | async-done | bytes 131088 | tf_op jit(solution)/shard_map/while/body/eval_jaxpr/psum | solution.py:15
  571.9 5.9 collective-permute-start
  578.7 2.9 collective-permute-start.1
  582.3 66.1 %all-reduce.5.cloned.1.call-done = f32[512,64]{0,1:T(8,128)} async-done(((f32[512,64]{0,1:T(8,128)}), f32[512,64]{0,1:T(8,128)}) %all-reduce.5.cloned.1.call-update) | async-done | bytes 131088 | tf_op jit(solution)/shard_map/while/body/eval_jaxpr/psum | solution.py:15
  656.0 5.9 collective-permute-start
  666.4 66.1 %all-reduce.5.cloned.1.call-done = f32[512,64]{0,1:T(8,128)} async-done(((f32[512,64]{0,1:T(8,128)}), f32[512,64]{0,1:T(8,128)}) %all-reduce.5.cloned.1.call-update) | async-done | bytes 131088 | tf_op jit(solution)/shard_map/while/body/eval_jaxpr/psum | solution.py:15
  740.1 5.9 collective-permute-start
  750.5 66.1 %all-reduce.5.cloned.1.call-done = f32[512,64]{0,1:T(8,128)} async-done(((f32[512,64]{0,1:T(8,128)}), f32[512,64]{0,1:T(8,128)}) %all-reduce.5.cloned.1.call-update) | async-done | bytes 131088 | tf_op jit(solution)/shard_map/while/body/eval_jaxpr/psum | solution.py:15
  824.2 5.9 collective-permute-start
  831.0 2.9 collective-permute-start.1
  834.6 65.8 %all-reduce.5.cloned.1.call-done = f32[512,64]{0,1:T(8,128)} async-done(((f32[512,64]{0,1:T(8,128)}), f32[512,64]{0,1:T(8,128)}) %all-reduce.5.cloned.1.call-update) | async-done | bytes 131088 | tf_op jit(solution)/shard_map/while/body/eval_jaxpr/psum | solution.py:15
  908.0 5.9 collective-permute-start
  918.5 66.1 %all-reduce.5.cloned.1.call-done = f32[512,64]{0,1:T(8,128)} async-done(((f32[512,64]{0,1:T(8,128)}), f32[512,64]{0,1:T(8,128)}) %all-reduce.5.cloned.1.call-update) | async-done | bytes 131088 | tf_op jit(solution)/shard_map/while/body/eval_jaxpr/psum | solution.py:15
  992.1 5.9 collective-permute-start
  999.0 2.9 collective-permute-start.1
  1002.5 65.7 %all-reduce.5.cloned.1.call-done = f32[512,64]{0,1:T(8,128)} async-done(((f32[512,64]{0,1:T(8,128)}), f32[512,64]{0,1:T(8,128)}) %all-reduce.5.cloned.1.call-update) | async-done | bytes 131088 | tf_op jit(solution)/shard_map/while/body/eval_jaxpr/psum | solution.py:15
  1075.9 5.9 collective-permute-start
  1082.7 2.9 collective-permute-start.1
  1086.3 66.1 %all-reduce.5.cloned.1.call-done = f32[512,64]{0,1:T(8,128)} async-done(((f32[512,64]{0,1:T(8,128)}), f32[512,64]{0,1:T(8,128)}) %all-reduce.5.cloned.1.call-update) | async-done | bytes 131088 | tf_op jit(solution)/shard_map/while/body/eval_jaxpr/psum | solution.py:15
  1160.0 5.9 collective-permute-start
  1166.8 2.9 collective-permute-start.1
  1170.4 65.7 %all-reduce.5.cloned.1.call-done = f32[512,64]{0,1:T(8,128)} async-done(((f32[512,64]{0,1:T(8,128)}), f32[512,64]{0,1:T(8,128)}) %all-reduce.5.cloned.1.call-update) | async-done | bytes 131088 | tf_op jit(solution)/shard_map/while/body/eval_jaxpr/psum | solution.py:15
  1243.8 5.9 collective-permute-start
  1250.6 2.9 collective-permute-start.1
  1254.2 65.8 %all-reduce.5.cloned.1.call-done = f32[512,64]{0,1:T(8,128)} async-done(((f32[512,64]{0,1:T(8,128)}), f32[512,64]{0,1:T(8,128)}) %all-reduce.5.cloned.1.call-update) | async-done | bytes 131088 | tf_op jit(solution)/shard_map/while/body/eval_jaxpr/psum | solution.py:15
  1327.7 5.9 collective-permute-start
  1338.1 65.7 %all-reduce.5.cloned.1.call-done = f32[512,64]{0,1:T(8,128)} async-done(((f32[512,64]{0,1:T(8,128)}), f32[512,64]{0,1:T(8,128)}) %all-reduce.5.cloned.1.call-update) | async-done | bytes 131088 | tf_op jit(solution)/shard_map/while/body/eval_jaxpr/psum | solution.py:15
  1412.2 74.9 %all-reduce.3.cloned.1.call-done = f32[512,64]{0,1:T(8,128)} async-done(((f32[512,64]{0,1:T(8,128)}), f32[512,64]{0,1:T(8,128)}) %all-reduce.3.cloned.1.call-update) | async-done | bytes 131088 | tf_op jit(solution)/shard_map/psum | solution.py:15
  1490.1 25.8 %psum.34 = f32[17,2]{1,0:T(8,128)S(1)} all-reduce(f32[17,2]{1,0:T(8,128)S(1)} %scatter.7), channel_id=1, replica_groups=mesh['skill'=64,'tensor'=8] {'tensor'}, use_global_device_ids=true, to_apply=%region_12.13 | all-reduce | flops 34 | bytes 272 | tf_op jit(solution)/shard_map/psum | solution.py:67
  (231 shorter events, 183.3 us)
Async XLA Ops:
  56.2 88.4 %all-reduce.5.cloned.1.call-start = ((), (), s32[]{:S(2)}) async-start(), calls=%async_computation.1 | async-start | bytes 262144 | tf_op jit(solution)/shard_map/while/body/eval_jaxpr/psum | solution.py:15
  59.5 89.3 %collective-permute-start = (bf16[1024,64]{1,0:T(8,128)(2,1)S(1)}, bf16[1024,64]{1,0:T(8,128)(2,1)}, u32[]{:S(2)}, u32[]{:S(2)}) collective-permute-start(bf16[1024,64]{1,0:T(8,128)(2,1)S(1)} %copy.18), channel_id=1, source_target_pairs={{8,0},{16,8},{24,16},{32,24},{40,32},{48,40},{56,48},{64,56},{72,6... | collective-permute-start | bytes 393224 | tf_op jit(solution)/shard_map/while/body/eval_jaxpr/ppermute | solution.py:10
  71.7 77.1 %collective-permute-start.1 = (bf16[64,1920]{1,0:T(8,128)(2,1)S(1)}, bf16[64,1920]{1,0:T(8,128)(2,1)}, u32[]{:S(2)}, u32[]{:S(2)}) collective-permute-start(bf16[64,1920]{1,0:T(8,128)(2,1)S(1)} %copy.19), channel_id=1, source_target_pairs={{8,0},{16,8},{24,16},{32,24},{40,32},{48,40},{56,48},{64,56},{72,6... | collective-permute-start | bytes 737288 | tf_op jit(solution)/shard_map/while/body/eval_jaxpr/ppermute | solution.py:10
  148.9 79.9 %all-reduce.5.cloned.1.call-start = ((), (), s32[]{:S(2)}) async-start(), calls=%async_computation.1 | async-start | bytes 262144 | tf_op jit(solution)/shard_map/while/body/eval_jaxpr/psum | solution.py:15
  152.2 80.8 %collective-permute-start = (bf16[1024,64]{1,0:T(8,128)(2,1)S(1)}, bf16[1024,64]{1,0:T(8,128)(2,1)}, u32[]{:S(2)}, u32[]{:S(2)}) collective-permute-start(bf16[1024,64]{1,0:T(8,128)(2,1)S(1)} %copy.18), channel_id=1, source_target_pairs={{8,0},{16,8},{24,16},{32,24},{40,32},{48,40},{56,48},{64,56},{72,6... | collective-permute-start | bytes 393224 | tf_op jit(solution)/shard_map/while/body/eval_jaxpr/ppermute | solution.py:10
  159.0 74.0 %collective-permute-start.1 = (bf16[64,1920]{1,0:T(8,128)(2,1)S(1)}, bf16[64,1920]{1,0:T(8,128)(2,1)}, u32[]{:S(2)}, u32[]{:S(2)}) collective-permute-start(bf16[64,1920]{1,0:T(8,128)(2,1)S(1)} %copy.19), channel_id=1, source_target_pairs={{8,0},{16,8},{24,16},{32,24},{40,32},{48,40},{56,48},{64,56},{72,6... | collective-permute-start | bytes 737288 | tf_op jit(solution)/shard_map/while/body/eval_jaxpr/ppermute | solution.py:10
  233.0 79.9 %all-reduce.5.cloned.1.call-start = ((), (), s32[]{:S(2)}) async-start(), calls=%async_computation.1 | async-start | bytes 262144 | tf_op jit(solution)/shard_map/while/body/eval_jaxpr/psum | solution.py:15
  236.4 80.8 %collective-permute-start = (bf16[1024,64]{1,0:T(8,128)(2,1)S(1)}, bf16[1024,64]{1,0:T(8,128)(2,1)}, u32[]{:S(2)}, u32[]{:S(2)}) collective-permute-start(bf16[1024,64]{1,0:T(8,128)(2,1)S(1)} %copy.18), channel_id=1, source_target_pairs={{8,0},{16,8},{24,16},{32,24},{40,32},{48,40},{56,48},{64,56},{72,6... | collective-permute-start | bytes 393224 | tf_op jit(solution)/shard_map/while/body/eval_jaxpr/ppermute | solution.py:10
  243.2 74.0 %collective-permute-start.1 = (bf16[64,1920]{1,0:T(8,128)(2,1)S(1)}, bf16[64,1920]{1,0:T(8,128)(2,1)}, u32[]{:S(2)}, u32[]{:S(2)}) collective-permute-start(bf16[64,1920]{1,0:T(8,128)(2,1)S(1)} %copy.19), channel_id=1, source_target_pairs={{8,0},{16,8},{24,16},{32,24},{40,32},{48,40},{56,48},{64,56},{72,6... | collective-permute-start | bytes 737288 | tf_op jit(solution)/shard_map/while/body/eval_jaxpr/ppermute | solution.py:10
  317.2 79.5 %all-reduce.5.cloned.1.call-start = ((), (), s32[]{:S(2)}) async-start(), calls=%async_computation.1 | async-start | bytes 262144 | tf_op jit(solution)/shard_map/while/body/eval_jaxpr/psum | solution.py:15
  320.6 80.4 %collective-permute-start = (bf16[1024,64]{1,0:T(8,128)(2,1)S(1)}, bf16[1024,64]{1,0:T(8,128)(2,1)}, u32[]{:S(2)}, u32[]{:S(2)}) collective-permute-start(bf16[1024,64]{1,0:T(8,128)(2,1)S(1)} %copy.18), channel_id=1, source_target_pairs={{8,0},{16,8},{24,16},{32,24},{40,32},{48,40},{56,48},{64,56},{72,6... | collective-permute-start | bytes 393224 | tf_op jit(solution)/shard_map/while/body/eval_jaxpr/ppermute | solution.py:10
  327.4 73.6 %collective-permute-start.1 = (bf16[64,1920]{1,0:T(8,128)(2,1)S(1)}, bf16[64,1920]{1,0:T(8,128)(2,1)}, u32[]{:S(2)}, u32[]{:S(2)}) collective-permute-start(bf16[64,1920]{1,0:T(8,128)(2,1)S(1)} %copy.19), channel_id=1, source_target_pairs={{8,0},{16,8},{24,16},{32,24},{40,32},{48,40},{56,48},{64,56},{72,6... | collective-permute-start | bytes 737288 | tf_op jit(solution)/shard_map/while/body/eval_jaxpr/ppermute | solution.py:10
  401.0 79.5 %all-reduce.5.cloned.1.call-start = ((), (), s32[]{:S(2)}) async-start(), calls=%async_computation.1 | async-start | bytes 262144 | tf_op jit(solution)/shard_map/while/body/eval_jaxpr/psum | solution.py:15
  404.3 80.4 %collective-permute-start = (bf16[1024,64]{1,0:T(8,128)(2,1)S(1)}, bf16[1024,64]{1,0:T(8,128)(2,1)}, u32[]{:S(2)}, u32[]{:S(2)}) collective-permute-start(bf16[1024,64]{1,0:T(8,128)(2,1)S(1)} %copy.18), channel_id=1, source_target_pairs={{8,0},{16,8},{24,16},{32,24},{40,32},{48,40},{56,48},{64,56},{72,6... | collective-permute-start | bytes 393224 | tf_op jit(solution)/shard_map/while/body/eval_jaxpr/ppermute | solution.py:10
  411.2 73.6 %collective-permute-start.1 = (bf16[64,1920]{1,0:T(8,128)(2,1)S(1)}, bf16[64,1920]{1,0:T(8,128)(2,1)}, u32[]{:S(2)}, u32[]{:S(2)}) collective-permute-start(bf16[64,1920]{1,0:T(8,128)(2,1)S(1)} %copy.19), channel_id=1, source_target_pairs={{8,0},{16,8},{24,16},{32,24},{40,32},{48,40},{56,48},{64,56},{72,6... | collective-permute-start | bytes 737288 | tf_op jit(solution)/shard_map/while/body/eval_jaxpr/ppermute | solution.py:10
  484.8 79.5 %all-reduce.5.cloned.1.call-start = ((), (), s32[]{:S(2)}) async-start(), calls=%async_computation.1 | async-start | bytes 262144 | tf_op jit(solution)/shard_map/while/body/eval_jaxpr/psum | solution.py:15
  488.1 80.4 %collective-permute-start = (bf16[1024,64]{1,0:T(8,128)(2,1)S(1)}, bf16[1024,64]{1,0:T(8,128)(2,1)}, u32[]{:S(2)}, u32[]{:S(2)}) collective-permute-start(bf16[1024,64]{1,0:T(8,128)(2,1)S(1)} %copy.18), channel_id=1, source_target_pairs={{8,0},{16,8},{24,16},{32,24},{40,32},{48,40},{56,48},{64,56},{72,6... | collective-permute-start | bytes 393224 | tf_op jit(solution)/shard_map/while/body/eval_jaxpr/ppermute | solution.py:10
  494.9 73.6 %collective-permute-start.1 = (bf16[64,1920]{1,0:T(8,128)(2,1)S(1)}, bf16[64,1920]{1,0:T(8,128)(2,1)}, u32[]{:S(2)}, u32[]{:S(2)}) collective-permute-start(bf16[64,1920]{1,0:T(8,128)(2,1)S(1)} %copy.19), channel_id=1, source_target_pairs={{8,0},{16,8},{24,16},{32,24},{40,32},{48,40},{56,48},{64,56},{72,6... | collective-permute-start | bytes 737288 | tf_op jit(solution)/shard_map/while/body/eval_jaxpr/ppermute | solution.py:10
  568.6 79.8 %all-reduce.5.cloned.1.call-start = ((), (), s32[]{:S(2)}) async-start(), calls=%async_computation.1 | async-start | bytes 262144 | tf_op jit(solution)/shard_map/while/body/eval_jaxpr/psum | solution.py:15
  571.9 80.7 %collective-permute-start = (bf16[1024,64]{1,0:T(8,128)(2,1)S(1)}, bf16[1024,64]{1,0:T(8,128)(2,1)}, u32[]{:S(2)}, u32[]{:S(2)}) collective-permute-start(bf16[1024,64]{1,0:T(8,128)(2,1)S(1)} %copy.18), channel_id=1, source_target_pairs={{8,0},{16,8},{24,16},{32,24},{40,32},{48,40},{56,48},{64,56},{72,6... | collective-permute-start | bytes 393224 | tf_op jit(solution)/shard_map/while/body/eval_jaxpr/ppermute | solution.py:10
  578.7 73.9 %collective-permute-start.1 = (bf16[64,1920]{1,0:T(8,128)(2,1)S(1)}, bf16[64,1920]{1,0:T(8,128)(2,1)}, u32[]{:S(2)}, u32[]{:S(2)}) collective-permute-start(bf16[64,1920]{1,0:T(8,128)(2,1)S(1)} %copy.19), channel_id=1, source_target_pairs={{8,0},{16,8},{24,16},{32,24},{40,32},{48,40},{56,48},{64,56},{72,6... | collective-permute-start | bytes 737288 | tf_op jit(solution)/shard_map/while/body/eval_jaxpr/ppermute | solution.py:10
  652.7 79.8 %all-reduce.5.cloned.1.call-start = ((), (), s32[]{:S(2)}) async-start(), calls=%async_computation.1 | async-start | bytes 262144 | tf_op jit(solution)/shard_map/while/body/eval_jaxpr/psum | solution.py:15
  656.0 80.7 %collective-permute-start = (bf16[1024,64]{1,0:T(8,128)(2,1)S(1)}, bf16[1024,64]{1,0:T(8,128)(2,1)}, u32[]{:S(2)}, u32[]{:S(2)}) collective-permute-start(bf16[1024,64]{1,0:T(8,128)(2,1)S(1)} %copy.18), channel_id=1, source_target_pairs={{8,0},{16,8},{24,16},{32,24},{40,32},{48,40},{56,48},{64,56},{72,6... | collective-permute-start | bytes 393224 | tf_op jit(solution)/shard_map/while/body/eval_jaxpr/ppermute | solution.py:10
  662.8 73.9 %collective-permute-start.1 = (bf16[64,1920]{1,0:T(8,128)(2,1)S(1)}, bf16[64,1920]{1,0:T(8,128)(2,1)}, u32[]{:S(2)}, u32[]{:S(2)}) collective-permute-start(bf16[64,1920]{1,0:T(8,128)(2,1)S(1)} %copy.19), channel_id=1, source_target_pairs={{8,0},{16,8},{24,16},{32,24},{40,32},{48,40},{56,48},{64,56},{72,6... | collective-permute-start | bytes 737288 | tf_op jit(solution)/shard_map/while/body/eval_jaxpr/ppermute | solution.py:10
  736.7 79.8 %all-reduce.5.cloned.1.call-start = ((), (), s32[]{:S(2)}) async-start(), calls=%async_computation.1 | async-start | bytes 262144 | tf_op jit(solution)/shard_map/while/body/eval_jaxpr/psum | solution.py:15
  740.1 80.7 %collective-permute-start = (bf16[1024,64]{1,0:T(8,128)(2,1)S(1)}, bf16[1024,64]{1,0:T(8,128)(2,1)}, u32[]{:S(2)}, u32[]{:S(2)}) collective-permute-start(bf16[1024,64]{1,0:T(8,128)(2,1)S(1)} %copy.18), channel_id=1, source_target_pairs={{8,0},{16,8},{24,16},{32,24},{40,32},{48,40},{56,48},{64,56},{72,6... | collective-permute-start | bytes 393224 | tf_op jit(solution)/shard_map/while/body/eval_jaxpr/ppermute | solution.py:10
  746.9 73.9 %collective-permute-start.1 = (bf16[64,1920]{1,0:T(8,128)(2,1)S(1)}, bf16[64,1920]{1,0:T(8,128)(2,1)}, u32[]{:S(2)}, u32[]{:S(2)}) collective-permute-start(bf16[64,1920]{1,0:T(8,128)(2,1)S(1)} %copy.19), channel_id=1, source_target_pairs={{8,0},{16,8},{24,16},{32,24},{40,32},{48,40},{56,48},{64,56},{72,6... | collective-permute-start | bytes 737288 | tf_op jit(solution)/shard_map/while/body/eval_jaxpr/ppermute | solution.py:10
  820.8 79.6 %all-reduce.5.cloned.1.call-start = ((), (), s32[]{:S(2)}) async-start(), calls=%async_computation.1 | async-start | bytes 262144 | tf_op jit(solution)/shard_map/while/body/eval_jaxpr/psum | solution.py:15
  824.2 80.5 %collective-permute-start = (bf16[1024,64]{1,0:T(8,128)(2,1)S(1)}, bf16[1024,64]{1,0:T(8,128)(2,1)}, u32[]{:S(2)}, u32[]{:S(2)}) collective-permute-start(bf16[1024,64]{1,0:T(8,128)(2,1)S(1)} %copy.18), channel_id=1, source_target_pairs={{8,0},{16,8},{24,16},{32,24},{40,32},{48,40},{56,48},{64,56},{72,6... | collective-permute-start | bytes 393224 | tf_op jit(solution)/shard_map/while/body/eval_jaxpr/ppermute | solution.py:10
  831.0 73.7 %collective-permute-start.1 = (bf16[64,1920]{1,0:T(8,128)(2,1)S(1)}, bf16[64,1920]{1,0:T(8,128)(2,1)}, u32[]{:S(2)}, u32[]{:S(2)}) collective-permute-start(bf16[64,1920]{1,0:T(8,128)(2,1)S(1)} %copy.19), channel_id=1, source_target_pairs={{8,0},{16,8},{24,16},{32,24},{40,32},{48,40},{56,48},{64,56},{72,6... | collective-permute-start | bytes 737288 | tf_op jit(solution)/shard_map/while/body/eval_jaxpr/ppermute | solution.py:10
  904.7 79.8 %all-reduce.5.cloned.1.call-start = ((), (), s32[]{:S(2)}) async-start(), calls=%async_computation.1 | async-start | bytes 262144 | tf_op jit(solution)/shard_map/while/body/eval_jaxpr/psum | solution.py:15
  908.0 80.7 %collective-permute-start = (bf16[1024,64]{1,0:T(8,128)(2,1)S(1)}, bf16[1024,64]{1,0:T(8,128)(2,1)}, u32[]{:S(2)}, u32[]{:S(2)}) collective-permute-start(bf16[1024,64]{1,0:T(8,128)(2,1)S(1)} %copy.18), channel_id=1, source_target_pairs={{8,0},{16,8},{24,16},{32,24},{40,32},{48,40},{56,48},{64,56},{72,6... | collective-permute-start | bytes 393224 | tf_op jit(solution)/shard_map/while/body/eval_jaxpr/ppermute | solution.py:10
  914.9 73.9 %collective-permute-start.1 = (bf16[64,1920]{1,0:T(8,128)(2,1)S(1)}, bf16[64,1920]{1,0:T(8,128)(2,1)}, u32[]{:S(2)}, u32[]{:S(2)}) collective-permute-start(bf16[64,1920]{1,0:T(8,128)(2,1)S(1)} %copy.19), channel_id=1, source_target_pairs={{8,0},{16,8},{24,16},{32,24},{40,32},{48,40},{56,48},{64,56},{72,6... | collective-permute-start | bytes 737288 | tf_op jit(solution)/shard_map/while/body/eval_jaxpr/ppermute | solution.py:10
  988.8 79.5 %all-reduce.5.cloned.1.call-start = ((), (), s32[]{:S(2)}) async-start(), calls=%async_computation.1 | async-start | bytes 262144 | tf_op jit(solution)/shard_map/while/body/eval_jaxpr/psum | solution.py:15
  992.1 80.4 %collective-permute-start = (bf16[1024,64]{1,0:T(8,128)(2,1)S(1)}, bf16[1024,64]{1,0:T(8,128)(2,1)}, u32[]{:S(2)}, u32[]{:S(2)}) collective-permute-start(bf16[1024,64]{1,0:T(8,128)(2,1)S(1)} %copy.18), channel_id=1, source_target_pairs={{8,0},{16,8},{24,16},{32,24},{40,32},{48,40},{56,48},{64,56},{72,6... | collective-permute-start | bytes 393224 | tf_op jit(solution)/shard_map/while/body/eval_jaxpr/ppermute | solution.py:10
  999.0 73.6 %collective-permute-start.1 = (bf16[64,1920]{1,0:T(8,128)(2,1)S(1)}, bf16[64,1920]{1,0:T(8,128)(2,1)}, u32[]{:S(2)}, u32[]{:S(2)}) collective-permute-start(bf16[64,1920]{1,0:T(8,128)(2,1)S(1)} %copy.19), channel_id=1, source_target_pairs={{8,0},{16,8},{24,16},{32,24},{40,32},{48,40},{56,48},{64,56},{72,6... | collective-permute-start | bytes 737288 | tf_op jit(solution)/shard_map/while/body/eval_jaxpr/ppermute | solution.py:10
  1072.6 79.8 %all-reduce.5.cloned.1.call-start = ((), (), s32[]{:S(2)}) async-start(), calls=%async_computation.1 | async-start | bytes 262144 | tf_op jit(solution)/shard_map/while/body/eval_jaxpr/psum | solution.py:15
  1075.9 80.7 %collective-permute-start = (bf16[1024,64]{1,0:T(8,128)(2,1)S(1)}, bf16[1024,64]{1,0:T(8,128)(2,1)}, u32[]{:S(2)}, u32[]{:S(2)}) collective-permute-start(bf16[1024,64]{1,0:T(8,128)(2,1)S(1)} %copy.18), channel_id=1, source_target_pairs={{8,0},{16,8},{24,16},{32,24},{40,32},{48,40},{56,48},{64,56},{72,6... | collective-permute-start | bytes 393224 | tf_op jit(solution)/shard_map/while/body/eval_jaxpr/ppermute | solution.py:10
  1082.7 73.9 %collective-permute-start.1 = (bf16[64,1920]{1,0:T(8,128)(2,1)S(1)}, bf16[64,1920]{1,0:T(8,128)(2,1)}, u32[]{:S(2)}, u32[]{:S(2)}) collective-permute-start(bf16[64,1920]{1,0:T(8,128)(2,1)S(1)} %copy.19), channel_id=1, source_target_pairs={{8,0},{16,8},{24,16},{32,24},{40,32},{48,40},{56,48},{64,56},{72,6... | collective-permute-start | bytes 737288 | tf_op jit(solution)/shard_map/while/body/eval_jaxpr/ppermute | solution.py:10
  1156.7 79.5 %all-reduce.5.cloned.1.call-start = ((), (), s32[]{:S(2)}) async-start(), calls=%async_computation.1 | async-start | bytes 262144 | tf_op jit(solution)/shard_map/while/body/eval_jaxpr/psum | solution.py:15
  1160.0 80.4 %collective-permute-start = (bf16[1024,64]{1,0:T(8,128)(2,1)S(1)}, bf16[1024,64]{1,0:T(8,128)(2,1)}, u32[]{:S(2)}, u32[]{:S(2)}) collective-permute-start(bf16[1024,64]{1,0:T(8,128)(2,1)S(1)} %copy.18), channel_id=1, source_target_pairs={{8,0},{16,8},{24,16},{32,24},{40,32},{48,40},{56,48},{64,56},{72,6... | collective-permute-start | bytes 393224 | tf_op jit(solution)/shard_map/while/body/eval_jaxpr/ppermute | solution.py:10
  1166.8 73.6 %collective-permute-start.1 = (bf16[64,1920]{1,0:T(8,128)(2,1)S(1)}, bf16[64,1920]{1,0:T(8,128)(2,1)}, u32[]{:S(2)}, u32[]{:S(2)}) collective-permute-start(bf16[64,1920]{1,0:T(8,128)(2,1)S(1)} %copy.19), channel_id=1, source_target_pairs={{8,0},{16,8},{24,16},{32,24},{40,32},{48,40},{56,48},{64,56},{72,6... | collective-permute-start | bytes 737288 | tf_op jit(solution)/shard_map/while/body/eval_jaxpr/ppermute | solution.py:10
  1240.5 79.6 %all-reduce.5.cloned.1.call-start = ((), (), s32[]{:S(2)}) async-start(), calls=%async_computation.1 | async-start | bytes 262144 | tf_op jit(solution)/shard_map/while/body/eval_jaxpr/psum | solution.py:15
  1243.8 80.5 %collective-permute-start = (bf16[1024,64]{1,0:T(8,128)(2,1)S(1)}, bf16[1024,64]{1,0:T(8,128)(2,1)}, u32[]{:S(2)}, u32[]{:S(2)}) collective-permute-start(bf16[1024,64]{1,0:T(8,128)(2,1)S(1)} %copy.18), channel_id=1, source_target_pairs={{8,0},{16,8},{24,16},{32,24},{40,32},{48,40},{56,48},{64,56},{72,6... | collective-permute-start | bytes 393224 | tf_op jit(solution)/shard_map/while/body/eval_jaxpr/ppermute | solution.py:10
  1250.6 73.7 %collective-permute-start.1 = (bf16[64,1920]{1,0:T(8,128)(2,1)S(1)}, bf16[64,1920]{1,0:T(8,128)(2,1)}, u32[]{:S(2)}, u32[]{:S(2)}) collective-permute-start(bf16[64,1920]{1,0:T(8,128)(2,1)S(1)} %copy.19), channel_id=1, source_target_pairs={{8,0},{16,8},{24,16},{32,24},{40,32},{48,40},{56,48},{64,56},{72,6... | collective-permute-start | bytes 737288 | tf_op jit(solution)/shard_map/while/body/eval_jaxpr/ppermute | solution.py:10
  1324.3 79.5 %all-reduce.5.cloned.1.call-start = ((), (), s32[]{:S(2)}) async-start(), calls=%async_computation.1 | async-start | bytes 262144 | tf_op jit(solution)/shard_map/while/body/eval_jaxpr/psum | solution.py:15
  1327.7 80.4 %collective-permute-start = (bf16[1024,64]{1,0:T(8,128)(2,1)S(1)}, bf16[1024,64]{1,0:T(8,128)(2,1)}, u32[]{:S(2)}, u32[]{:S(2)}) collective-permute-start(bf16[1024,64]{1,0:T(8,128)(2,1)S(1)} %copy.18), channel_id=1, source_target_pairs={{8,0},{16,8},{24,16},{32,24},{40,32},{48,40},{56,48},{64,56},{72,6... | collective-permute-start | bytes 393224 | tf_op jit(solution)/shard_map/while/body/eval_jaxpr/ppermute | solution.py:10
  1408.1 79.0 %all-reduce.3.cloned.1.call-start = ((), (), s32[]{:S(2)}) async-start(), calls=%async_computation | async-start | bytes 262144 | tf_op jit(solution)/shard_map/psum | solution.py:15
  (8 other events, 169.3 us)
Sparse Core Ops, SparseCore 0:
  60.2 84.3 all-reduce.4
  152.9 75.8 all-reduce.4
  237.0 75.8 all-reduce.4
  320.9 75.7 all-reduce.4
  404.7 75.7 all-reduce.4
  488.5 75.7 all-reduce.4
  572.6 75.7 all-reduce.4
  656.6 75.7 all-reduce.4
  740.7 75.7 all-reduce.4
  824.5 75.8 all-reduce.4
  908.7 75.7 all-reduce.4
  992.5 75.7 all-reduce.4
  1076.6 75.7 all-reduce.4
  1160.3 75.7 all-reduce.4
  1244.1 75.8 all-reduce.4
  1328.0 75.7 all-reduce.4
Sparse Core Ops, SparseCore 1:
  1411.5 75.6 all-reduce.2
where the time goes:
time: 1530 us
  waiting for transfers between devices  1140 us (75%)
  starting transfers between devices  151 us (10%)
  matrix products  69.7 us (5%)
  other arithmetic  57.7 us (4%)
  blocking collectives  54 us (4%)
  local copies, waits for them, and re-layouts  36 us (2%)
  between operations  16.6 us (1%)
    psum x17, waiting for transfers between devices, evaluate(): summed = lax.psum(partial_value, 'tensor')  1130 us
    ppermute x34, starting transfers between devices, from_behind(): return lax.ppermute(block, axis, route)  150 us
    another operation x33, other arithmetic  42.9 us
    dot_general x17, matrix products, evaluate(): jnp.dot(valid_act, down_piece, preferred_element_type=jnp.float32)  39.4 us
  transfers between devices with their start and end apart: 51, of which 18 were waited for; matrix products, arithmetic and copies ran while one was open for 6% of the time, Pallas kernels for 0%

commit v1 on v0

v1 whole, which is shorter than its diff:
```python
import functools

import jax
import jax.numpy as jnp
from jax import lax
from jax.experimental import pallas as pl
from jax.experimental.pallas import tpu as pltpu
from jax.sharding import PartitionSpec as P

F32 = jnp.float32
BF16 = jnp.bfloat16
STEPS = 4
CHIPS = 4
CORES = 2
GROUP = 8
NT = (((1,), (1,)), ((), ()))


def kernel(
    skills,
    reach,
    act_hbm,
    cot_hbm,
    index_ref,
    vact_hbm,
    vcot_hbm,
    label_ref,
    down_hbm,
    own_out,
    other_out,
    act,
    cot,
    vact,
    vcot,
    down_raw,
    down_own,
    down_all,
    up_own,
    up_all,
    part,
    part_in,
    share,
    full,
    send_f32,
    core_in,
    chip_out,
    chip_in,
    keep,
    own_f32,
    own_core_in,
    own_chip_out,
    own_chip_in,
    own_keep,
    table,
    table_in,
    load_sem,
    send_sem,
    recv_sem,
):
    me = lax.axis_index("skill")
    lane_pos = lax.axis_index("tensor")
    chip = lane_pos // CORES
    core = lax.rem(lane_pos, CORES)
    rank = down_own.shape[0]
    train = act.shape[0]
    piece = rank // CORES

    loads = []
    for n, (src, dst) in enumerate(
        [(down_hbm, down_raw), (act_hbm, act), (vact_hbm, vact), (cot_hbm, cot), (vcot_hbm, vcot)]
    ):
        copy = pltpu.make_async_copy(src, dst, load_sem.at[n])
        copy.start()
        loads.append(copy)
    load_down, load_act, load_vact, load_cot, load_vcot = loads

    def skill_at(shift):
        return (lax.rem(me + shift + skills, skills), lane_pos)

    def tensor_at(shift):
        return (me, lax.rem(lane_pos + shift, GROUP))

    def chip_at(shift):
        return (me, lax.rem(chip + shift, CHIPS) * CORES + core)

    sibling = (me, chip * CORES + (1 - core))

    barrier = pltpu.get_barrier_semaphore()
    partners = [skill_at(d) for d in (1, -1, reach, -reach)]
    partners += [tensor_at(d) for d in range(1, GROUP)]
    for partner in partners:
        pl.semaphore_signal(
            barrier, inc=1, device_id=partner, device_id_type=pl.DeviceIdType.MESH
        )

    started = []

    def send(src, dst, target):
        n = len(started)
        copy = pltpu.make_async_remote_copy(
            src_ref=src,
            dst_ref=dst,
            send_sem=send_sem.at[n],
            recv_sem=recv_sem.at[n],
            device_id=target,
            device_id_type=pl.DeviceIdType.MESH,
        )
        copy.start()
        started.append(copy)
        return copy

    def relay(own, held, step):
        def block(way):
            if step == 0:
                return own
            return held.at[step - 1, pl.ds(way * rank, rank)]

        def slot(way):
            return held.at[step, pl.ds(way * rank, rank)]

        return (
            send(block(0), slot(0), skill_at(1)),
            send(block(1), slot(1), skill_at(-1)),
            send(block(0), slot(2), skill_at(-reach)),
            send(block(1), slot(3), skill_at(reach)),
        )

    def near(copies):
        copies[0].wait_recv()
        copies[1].wait_recv()

    def far(copies):
        copies[2].wait_recv()
        copies[3].wait_recv()

    def scatter_cores(unit, product):
        rows = product.reshape(CHIPS, CORES, piece, product.shape[1])
        for c in range(CORES):
            send_f32[unit, c] = rows[:, c]
        return send(send_f32.at[unit, 1 - core], core_in.at[unit], sibling)

    def scatter_chips(unit, copy):
        copy.wait_recv()
        summed = send_f32[unit, core] + core_in[unit]
        chip_out[unit] = summed.astype(BF16)
        keep[unit] = summed
        return [
            send(
                chip_out.at[unit, lax.rem(chip + d, CHIPS)],
                chip_in.at[unit, d - 1],
                chip_at(d),
            )
            for d in range(1, CHIPS)
        ]

    def total(unit, copies):
        for copy in copies:
            copy.wait_recv()
        value = keep[unit, chip]
        for d in range(CHIPS - 1):
            value = value + chip_in[unit, d].astype(F32)
        return value

    load_down.wait()
    spot = lax.broadcasted_iota(jnp.int32, (rank, rank), 0)
    across = lax.broadcasted_iota(jnp.int32, (rank, rank), 1)
    eye = jnp.where(spot == across, 1.0, 0.0).astype(BF16)
    down_own[...] = lax.dot_general(
        eye, down_raw[...], NT, preferred_element_type=F32
    ).astype(BF16)
    pl.semaphore_wait(barrier, len(partners))
    down_moves = [relay(down_own, down_all, 0)]

    load_act.wait()
    part[...] = lax.dot_general(
        down_own[...], act[...], NT, preferred_element_type=F32
    ).reshape(part.shape)
    part_moves = [
        send(part.at[lax.rem(lane_pos + d, GROUP)], part_in.at[d - 1], tensor_at(d))
        for d in range(1, GROUP)
    ]
    load_vact.wait()
    own_val = lax.dot_general(down_own[...], vact[...], NT, preferred_element_type=F32)
    for copy in part_moves:
        copy.wait_recv()
    summed = part[lane_pos]
    for d in range(GROUP - 1):
        summed = summed + part_in[d]
    share[...] = summed
    full[lane_pos] = summed
    full_moves = [send(share, full.at[lane_pos], tensor_at(d)) for d in range(1, GROUP)]

    near(down_moves[0])
    down_moves.append(relay(down_own, down_all, 1))

    stored = lax.broadcasted_iota(jnp.int32, (train, train), 0)
    hits = jnp.where(stored == index_ref[...], 1.0, 0.0).astype(BF16)
    counts = lax.dot_general(
        jnp.ones((8, train), BF16), hits, NT, preferred_element_type=F32
    )[0:1]

    load_cot.wait()
    for copy in full_moves:
        copy.wait_recv()
    proj = full[...].reshape(rank, train).astype(BF16).astype(F32)
    weighted = proj * counts
    high = weighted.astype(BF16)
    low = (weighted - high.astype(F32)).astype(BF16)
    product = jnp.dot(
        jnp.concatenate([high, low], axis=0), cot[...], preferred_element_type=F32
    )
    up_own[...] = ((product[:rank] + product[rank:]) * (-1.0 / train)).astype(BF16)
    up_moves = [relay(up_own, up_all, 0)]

    def val_step(step):
        far(down_moves[step])
        return scatter_cores(
            step,
            lax.dot_general(down_all[step], vact[...], NT, preferred_element_type=F32),
        )

    def cot_step(step):
        far(up_moves[step])
        return scatter_cores(
            STEPS + step,
            lax.dot_general(up_all[step], vcot[...], NT, preferred_element_type=F32),
        )

    core_moves = {}
    chip_moves = {}
    core_moves[0] = val_step(0)
    near(down_moves[1])
    down_moves.append(relay(down_own, down_all, 2))

    load_vcot.wait()
    own_cot = lax.dot_general(up_own[...], vcot[...], NT, preferred_element_type=F32)
    for chip_n in range(CHIPS):
        for core_n in range(CORES):
            at = (chip_n * CORES + core_n) * (rank // GROUP)
            own_f32[core_n, chip_n, 0:8] = own_val[at : at + 8]
            own_f32[core_n, chip_n, 8:16] = own_cot[at : at + 8]
    own_core = send(own_f32.at[1 - core], own_core_in, sibling)
    chip_moves[0] = scatter_chips(0, core_moves[0])

    near(down_moves[2])
    down_moves.append(relay(down_own, down_all, 3))
    core_moves[1] = val_step(1)

    near(up_moves[0])
    up_moves.append(relay(up_own, up_all, 1))

    own_core.wait_recv()
    own_sum = own_f32[core] + own_core_in[...]
    own_chip_out[...] = own_sum.astype(BF16)
    own_keep[...] = own_sum
    own_chip = [
        send(own_chip_out.at[lax.rem(chip + d, CHIPS)], own_chip_in.at[d - 1], chip_at(d))
        for d in range(1, CHIPS)
    ]
    chip_moves[1] = scatter_chips(1, core_moves[1])
    core_moves[4] = cot_step(0)
    core_moves[2] = val_step(2)
    chip_moves[4] = scatter_chips(4, core_moves[4])
    chip_moves[2] = scatter_chips(2, core_moves[2])

    near(up_moves[1])
    up_moves.append(relay(up_own, up_all, 2))
    near(down_moves[3])
    core_moves[3] = val_step(3)
    core_moves[5] = cot_step(1)
    chip_moves[3] = scatter_chips(3, core_moves[3])
    chip_moves[5] = scatter_chips(5, core_moves[5])

    near(up_moves[2])
    up_moves.append(relay(up_own, up_all, 3))
    core_moves[6] = cot_step(2)
    chip_moves[6] = scatter_chips(6, core_moves[6])

    def change(step):
        value = total(step, chip_moves[step]) * total(
            STEPS + step, chip_moves[STEPS + step]
        )
        return jnp.sum(value, axis=0, keepdims=True)

    for copy in own_chip:
        copy.wait_recv()
    own_piece = own_keep[chip]
    for d in range(CHIPS - 1):
        own_piece = own_piece + own_chip_in[d].astype(F32)
    changes = [change(0), change(1)]
    own_change = jnp.sum(own_piece[0:8] * own_piece[8:16], axis=0, keepdims=True)

    near(up_moves[3])
    core_moves[7] = cot_step(3)
    chip_moves[7] = scatter_chips(7, core_moves[7])
    changes.append(change(2))
    changes.append(change(3))

    own_mask = (label_ref[...] == me).astype(F32)
    other_mask = 1.0 - own_mask
    stack = jnp.concatenate(
        changes + [own_change, jnp.zeros((3, own_change.shape[1]), F32)], axis=0
    )
    own_part = jnp.sum(stack * own_mask, axis=1, keepdims=True)
    other_part = jnp.sum(stack * other_mask, axis=1, keepdims=True)

    row = lax.broadcasted_iota(jnp.int32, (8, 128), 0)
    column = lax.broadcasted_iota(jnp.int32, (8, 128), 1)
    from_behind = chip == 0
    from_ahead = chip == 1
    from_far_ahead = chip == 2
    place = jnp.where(
        from_behind,
        reach - 1 - row,
        jnp.where(
            from_ahead, reach + 1 + row, jnp.where(from_far_ahead, 2 * reach - row, row)
        ),
    )
    place = jnp.where(row == STEPS, reach, place)
    chosen = (place == column) & (row <= STEPS)
    own_row = jnp.sum(jnp.where(chosen, own_part, 0.0), axis=0, keepdims=True)
    other_row = jnp.sum(jnp.where(chosen, other_part, 0.0), axis=0, keepdims=True)
    table[...] = jnp.where(row == 0, own_row, jnp.where(row == 1, other_row, 0.0))
    table_moves = [send(table, table_in.at[d - 1], tensor_at(d)) for d in range(1, GROUP)]
    own_count = jnp.maximum(jnp.sum(own_mask, axis=1, keepdims=True), 1.0)
    other_count = jnp.maximum(jnp.sum(other_mask, axis=1, keepdims=True), 1.0)
    for copy in table_moves:
        copy.wait_recv()
    result = jnp.zeros((8, 128), F32)
    for t in range(GROUP):
        away = lax.rem(lane_pos - t + GROUP, GROUP)
        theirs = table_in[lax.max(away - 1, 0)]
        result = result + jnp.where(away == 0, table[...], theirs)
    columns = own_out.shape[1]
    own_out[...] = result[0:1, :columns] / own_count
    other_out[...] = result[1:2, :columns] / other_count
    for copy in started:
        copy.wait_send()


def on_device(
    stored_inputs,
    stored_output_gradient,
    training_token_index,
    validation_inputs,
    validation_output_gradient,
    validation_row_skill,
    adapter_down_init,
):
    skills = lax.axis_size("skill")
    reach = skills // 8
    columns = 2 * reach + 1
    _, train, width = stored_inputs.shape
    hidden = stored_output_gradient.shape[2]
    rows = validation_inputs.shape[1]
    rank = adapter_down_init.shape[2]
    piece = rank // CORES
    units = 2 * STEPS
    copies = 2 * 4 * STEPS + 3 * (GROUP - 1) + units * CHIPS + CHIPS
    any_spec = pl.BlockSpec(memory_space=pl.ANY)
    vmem_spec = pl.BlockSpec(memory_space=pltpu.VMEM)
    return pl.pallas_call(
        functools.partial(kernel, skills, reach),
        out_shape=(
            jax.ShapeDtypeStruct((1, columns), F32),
            jax.ShapeDtypeStruct((1, columns), F32),
        ),
        in_specs=[any_spec, any_spec, vmem_spec, any_spec, any_spec, vmem_spec, any_spec],
        out_specs=(vmem_spec, vmem_spec),
        scratch_shapes=[
            pltpu.VMEM((train, width), BF16),
            pltpu.VMEM((train, hidden), BF16),
            pltpu.VMEM((rows, width), BF16),
            pltpu.VMEM((rows, hidden), BF16),
            pltpu.VMEM((width, rank), BF16),
            pltpu.VMEM((rank, width), BF16),
            pltpu.VMEM((STEPS, 4 * rank, width), BF16),
            pltpu.VMEM((rank, hidden), BF16),
            pltpu.VMEM((STEPS, 4 * rank, hidden), BF16),
            pltpu.VMEM((GROUP, rank // GROUP, train), F32),
            pltpu.VMEM((GROUP - 1, rank // GROUP, train), F32),
            pltpu.VMEM((rank // GROUP, train), F32),
            pltpu.VMEM((GROUP, rank // GROUP, train), F32),
            pltpu.VMEM((units, CORES, CHIPS, piece, rows), F32),
            pltpu.VMEM((units, CHIPS, piece, rows), F32),
            pltpu.VMEM((units, CHIPS, piece, rows), BF16),
            pltpu.VMEM((units, CHIPS - 1, piece, rows), BF16),
            pltpu.VMEM((units, CHIPS, piece, rows), F32),
            pltpu.VMEM((CORES, CHIPS, 16, rows), F32),
            pltpu.VMEM((CHIPS, 16, rows), F32),
            pltpu.VMEM((CHIPS, 16, rows), BF16),
            pltpu.VMEM((CHIPS - 1, 16, rows), BF16),
            pltpu.VMEM((CHIPS, 16, rows), F32),
            pltpu.VMEM((8, 128), F32),
            pltpu.VMEM((GROUP - 1, 8, 128), F32),
            pltpu.SemaphoreType.DMA((5,)),
            pltpu.SemaphoreType.DMA((copies,)),
            pltpu.SemaphoreType.DMA((copies,)),
        ],
        compiler_params=pltpu.CompilerParams(
            collective_id=0, has_side_effects=True, vmem_limit_bytes=48 * 1024 * 1024
        ),
    )(
        stored_inputs[0],
        stored_output_gradient[0],
        training_token_index,
        validation_inputs[0],
        validation_output_gradient[0],
        validation_row_skill,
        adapter_down_init[0],
    )


def solution(mesh):
    in_specs = (
        P("skill", None, "tensor"),
        P("skill", None, "tensor"),
        P("skill", None),
        P("skill", None, "tensor"),
        P("skill", None, "tensor"),
        P("skill", None),
        P("skill", "tensor", None),
    )
    out_specs = (P("skill", None), P("skill", None))
    return jax.shard_map(
        on_device, mesh=mesh, in_specs=in_specs, out_specs=out_specs, check_vma=False
    )
```

time: 1530 us -> 131 us (0.09)
  waiting for transfers between devices: 1140 us -> 0 us
  starting transfers between devices: 151 us -> 0 us
  Pallas kernels: 0 us -> 122 us
  matrix products: 69.7 us -> 0 us
  other arithmetic: 57.7 us -> 0 us
  blocking collectives: 54 us -> 0 us
  local copies, waits for them, and re-layouts: 36 us -> 8.46 us
  between operations: 16.6 us -> 0.66 us
    psum x17 -> x0, waiting for transfers between devices: 1130 us -> none  [evaluate(): summed = lax.psum(partial_value, 'tensor')]
    ppermute x34 -> x0, starting transfers between devices: 150 us -> none  [from_behind(): return lax.ppermute(block, axis, route)]
    pallas_call x0 -> x1, Pallas kernels: none -> 122 us  [on_device(): pl.pallas_call(functools.partial(kernel, skills, reach), out_shape=(jax.S...]
    dot_general x36 -> x0, matrix products: 69.7 us -> none  [the longest x17 39.4 us: evaluate(): jnp.dot(valid_act, down_piece, preferred_element_type=jnp.float32)]
    psum x2 -> x0, blocking collectives: 54 us -> none  [the longest x1 28.2 us: on_device(): proj = lax.psum(partial_value, 'tensor').astype(jnp.bfloat16)]
    another operation x33 -> x0, other arithmetic: 42.9 us -> none
    another operation x32 -> x0, local copies, waits for them, and re-layouts: 30.4 us -> none
  transfers between devices with their start and end apart: 51 -> 0, of which waited for: 18 -> 0; matrix products, arithmetic and copies ran while one was open for 6% -> 0% of each run, Pallas kernels for 0% -> 0%
where the time goes in v1:
time: 131 us
  Pallas kernels  122 us (93%)
  local copies, waits for them, and re-layouts  8.46 us (6%)
    pallas_call x1, Pallas kernels, on_device(): pl.pallas_call(functools.partial(kernel, skills, reach), out_shape=(jax.S...  122 us
    unnamed x15, local copies, waits for them, and re-layouts  8.46 us

profile of v1, /device:TPU:7, one launch (start us, length us, event | category | flops | bytes accessed | tf_op | source)
XLA Modules:
  0.0 131.1 jit_solution(12799821096235967869)
XLA Ops:
  0.6 1.1 copy.9
  1.7 0.0 copy-start
  1.7 1.5 %copy-done = bf16[1,512,1920]{2,1,0:T(8,128)(2,1)S(1)} copy-done((bf16[1,512,1920]{2,1,0:T(8,128)(2,1)S(1)}, bf16[1,512,1920]{2,1,0:T(8,128)(2,1)}, u32[]{:S(2)}) %copy-start) | copy-done | bytes 1966104
  3.3 0.0 copy-start.1
  3.3 1.2 copy-done.1
  4.5 0.0 copy-start.2
  4.5 1.2 copy-done.2
  5.7 0.0 copy-start.3
  5.7 1.0 copy-done.3
  6.7 0.0 copy-start.4
  6.7 0.7 copy-done.4
  7.4 0.0 copy-start.5
  7.4 0.7 copy-done.5
  8.1 121.9 %shard_map.86 = (f32[1,17]{1,0:T(1,128)S(1)}, f32[1,17]{1,0:T(1,128)S(1)}) custom-call(bf16[256,1024]{1,0:T(8,128)(2,1)S(1)} %bitcast.9, bf16[256,1920]{1,0:T(8,128)(2,1)S(1)} %bitcast.8, s32[1,256]{1,0:T(1,128)S(1)} %copy-done.5, bf16[512,1024]{1,0:T(8,128)(2,1)S(1)} %bitcast.6, bf16[512,1920]{1,0:T(8,128)(2,1)S(1)} %bitcast.5, s32[1,512]{1,0:T(1,128)S(1)} %copy-done.4, ...), custom_call_target="tpu_custom_call" | custom-call | tf_op jit(solution)/shard_map/pallas_call | solution.py:362
  130.0 0.5 copy.12
  130.6 0.5 copy.13
Async XLA Ops:
  1.7 1.6 %copy-start = (bf16[1,512,1920]{2,1,0:T(8,128)(2,1)S(1)}, bf16[1,512,1920]{2,1,0:T(8,128)(2,1)}, u32[]{:S(2)}) copy-start(bf16[1,512,1920]{2,1,0:T(8,128)(2,1)} %param.11) | copy-start | bytes 5898244
  3.3 1.2 copy-start.1
  4.5 1.2 copy-start.2
  5.7 1.0 copy-start.3
  6.7 0.7 copy-start.4
  7.4 0.7 copy-start.5

commit v2 on v1

--- a/solution.py
+++ b/solution.py
@@ -10,6 +10,7 @@
 F32 = jnp.float32
 BF16 = jnp.bfloat16
 STEPS = 4
+BLOCKS = 16
 CHIPS = 4
 CORES = 2
 GROUP = 8
@@ -32,11 +33,12 @@
     cot,
     vact,
     vcot,
-    down_raw,
     down_own,
     down_all,
     up_own,
     up_all,
+    tail_own,
+    tail_all,
     part,
     part_in,
     share,
@@ -56,6 +58,7 @@
     load_sem,
     send_sem,
     recv_sem,
+    block_sem,
 ):
     me = lax.axis_index("skill")
     lane_pos = lax.axis_index("tensor")
@@ -67,7 +70,7 @@
 
     loads = []
     for n, (src, dst) in enumerate(
-        [(down_hbm, down_raw), (act_hbm, act), (vact_hbm, vact), (cot_hbm, cot), (vcot_hbm, vcot)]
+        [(down_hbm, down_own), (act_hbm, act), (vact_hbm, vact), (cot_hbm, cot), (vcot_hbm, vcot)]
     ):
         copy = pltpu.make_async_copy(src, dst, load_sem.at[n])
         copy.start()
@@ -86,7 +89,13 @@
     sibling = (me, chip * CORES + (1 - core))
 
     barrier = pltpu.get_barrier_semaphore()
-    partners = [skill_at(d) for d in (1, -1, reach, -reach)]
+    depth = lax.rem(me, reach)
+    low_half = depth < reach // 2
+
+    def ring_at(shift):
+        return (me - depth + lax.rem(depth + shift + reach, reach), lane_pos)
+
+    partners = [ring_at(1), ring_at(-1), skill_at(reach), skill_at(-reach)]
     partners += [tensor_at(d) for d in range(1, GROUP)]
     for partner in partners:
         pl.semaphore_signal(
@@ -94,9 +103,10 @@
         )
 
     started = []
+    started_if = []
 
     def send(src, dst, target):
-        n = len(started)
+        n = len(started) + len(started_if)
         copy = pltpu.make_async_remote_copy(
             src_ref=src,
             dst_ref=dst,
@@ -109,29 +119,105 @@
         started.append(copy)
         return copy
 
-    def relay(own, held, step):
-        def block(way):
-            if step == 0:
-                return own
-            return held.at[step - 1, pl.ds(way * rank, rank)]
-
-        def slot(way):
-            return held.at[step, pl.ds(way * rank, rank)]
-
-        return (
-            send(block(0), slot(0), skill_at(1)),
-            send(block(1), slot(1), skill_at(-1)),
-            send(block(0), slot(2), skill_at(-reach)),
-            send(block(1), slot(3), skill_at(reach)),
-        )
-
-    def near(copies):
-        copies[0].wait_recv()
-        copies[1].wait_recv()
-
-    def far(copies):
-        copies[2].wait_recv()
-        copies[3].wait_recv()
+    class Stream:
+        def __init__(self, own, held):
+            self.own, self.held = own, held
+            self.base = len(streams) * BLOCKS
+            streams.append(self)
+
+        def block(self, slot):
+            return self.own if slot is None else self.held.at[slot]
+
+        def send(self, source, slot, target, when=None):
+            n = len(started) + len(started_if)
+            copy = pltpu.make_async_remote_copy(
+                src_ref=self.block(source),
+                dst_ref=self.held.at[slot],
+                send_sem=send_sem.at[n],
+                recv_sem=block_sem.at[self.base + slot],
+                device_id=target,
+                device_id_type=pl.DeviceIdType.MESH,
+            )
+            if when is None:
+                copy.start()
+                started.append(copy)
+            else:
+                pl.when(when)(copy.start)
+                started_if.append((when, copy))
+
+        def wait(self, *slots):
+            for slot in slots:
+                pltpu.make_async_remote_copy(
+                    src_ref=self.own,
+                    dst_ref=self.held.at[slot],
+                    send_sem=send_sem.at[0],
+                    recv_sem=block_sem.at[self.base + slot],
+                    device_id=sibling,
+                    device_id_type=pl.DeviceIdType.MESH,
+                ).wait_recv()
+
+        def step0(self):
+            self.send(None, 0, ring_at(1))
+            self.send(None, 1, ring_at(-1))
+            self.send(None, 2, skill_at(-reach))
+            self.send(None, 3, skill_at(reach))
+
+        def step1(self):
+            self.wait(0, 1)
+            self.send(0, 4, ring_at(1))
+            self.send(1, 5, ring_at(-1))
+            self.send(0, 6, skill_at(-reach), depth >= 1)
+            self.send(1, 7, skill_at(reach), depth <= reach - 2)
+
+        def wrap1(self):
+            self.wait(2, 3)
+            self.send(3, 6, ring_at(1), depth == reach - 1)
+            self.send(2, 7, ring_at(-1), depth == 0)
+
+        def step2(self):
+            self.wait(4, 5)
+            self.send(4, 8, ring_at(1))
+            self.send(5, 9, ring_at(-1))
+            self.send(4, jnp.where(low_half, 13, 10), skill_at(-reach), depth >= 2)
+            self.send(5, jnp.where(low_half, 10, 13), skill_at(reach), depth <= reach - 3)
+
+        def wrap2(self):
+            self.wait(6, 7)
+            self.send(6, 13, ring_at(1), depth == 0)
+            self.send(7, 13, ring_at(-1), depth == reach - 1)
+
+        def step3(self, ahead):
+            self.wait(8, 9)
+            if ahead:
+                self.send(8, 12, ring_at(1))
+            else:
+                self.send(9, 12, ring_at(-1))
+            self.send(8, jnp.where(low_half, 14, 11), skill_at(-reach), depth >= 3)
+            self.send(9, jnp.where(low_half, 11, 14), skill_at(reach), depth <= reach - 4)
+
+        def step4(self):
+            self.wait(12)
+            self.send(12, 15, skill_at(jnp.where(low_half, reach, -reach)))
+
+        def relay1(self):
+            self.wait(15)
+            self.send(
+                15,
+                14,
+                ring_at(jnp.where(low_half, -1, 1)),
+                (depth != 0) & (depth != reach - 1),
+            )
+
+        def relay2(self):
+            self.wait(14)
+            self.send(
+                14,
+                13,
+                ring_at(jnp.where(low_half, -1, 1)),
+                (depth == 1) | (depth == reach - 2),
+            )
+
+    streams = []
 
     def scatter_cores(unit, product):
         rows = product.reshape(CHIPS, CORES, piece, product.shape[1])
@@ -162,14 +248,12 @@
         return value
 
     load_down.wait()
-    spot = lax.broadcasted_iota(jnp.int32, (rank, rank), 0)
-    across = lax.broadcasted_iota(jnp.int32, (rank, rank), 1)
-    eye = jnp.where(spot == across, 1.0, 0.0).astype(BF16)
-    down_own[...] = lax.dot_general(
-        eye, down_raw[...], NT, preferred_element_type=F32
-    ).astype(BF16)
     pl.semaphore_wait(barrier, len(partners))
-    down_moves = [relay(down_own, down_all, 0)]
+    down = Stream(down_own, down_all)
+    up = Stream(up_own, up_all)
+    tail = Stream(tail_own, tail_all)
+    split = up_own.shape[1]
+    down.step0()
 
     load_act.wait()
     part[...] = lax.dot_general(
@@ -190,8 +274,8 @@
     full[lane_pos] = summed
     full_moves = [send(share, full.at[lane_pos], tensor_at(d)) for d in range(1, GROUP)]
 
-    near(down_moves[0])
-    down_moves.append(relay(down_own, down_all, 1))
+    down.step1()
+    down.wrap1()
 
     stored = lax.broadcasted_iota(jnp.int32, (train, train), 0)
     hits = jnp.where(stored == index_ref[...], 1.0, 0.0).astype(BF16)
@@ -209,31 +293,38 @@
     product = jnp.dot(
         jnp.concatenate([high, low], axis=0), cot[...], preferred_element_type=F32
     )
-    up_own[...] = ((product[:rank] + product[rank:]) * (-1.0 / train)).astype(BF16)
-    up_moves = [relay(up_own, up_all, 0)]
-
-    def val_step(step):
-        far(down_moves[step])
+    factor = ((product[:rank] + product[rank:]) * (-1.0 / train)).astype(BF16)
+    up_own[...] = factor[:, :split]
+    up.step0()
+    tail_own[...] = factor[:, split:]
+    tail.step0()
+    down.step2()
+
+    def val_step(unit):
+        rows = down_all[4 * unit : 4 * unit + 4].reshape(4 * rank, down_own.shape[1])
         return scatter_cores(
-            step,
-            lax.dot_general(down_all[step], vact[...], NT, preferred_element_type=F32),
+            unit, lax.dot_general(rows, vact[...], NT, preferred_element_type=F32)
         )
 
-    def cot_step(step):
-        far(up_moves[step])
-        return scatter_cores(
-            STEPS + step,
-            lax.dot_general(up_all[step], vcot[...], NT, preferred_element_type=F32),
-        )
+    def cot_dot(first, second):
+        return lax.dot_general(
+            first, vcot[:, :split], NT, preferred_element_type=F32
+        ) + lax.dot_general(second, vcot[:, split:], NT, preferred_element_type=F32)
+
+    def cot_step(unit):
+        rows = up_all[4 * unit : 4 * unit + 4].reshape(4 * rank, split)
+        rest = tail_all[4 * unit : 4 * unit + 4].reshape(4 * rank, tail_own.shape[1])
+        return scatter_cores(STEPS + unit, cot_dot(rows, rest))
 
     core_moves = {}
     chip_moves = {}
     core_moves[0] = val_step(0)
-    near(down_moves[1])
-    down_moves.append(relay(down_own, down_all, 2))
+    down.wrap2()
+    up.step1()
+    tail.step1()
 
     load_vcot.wait()
-    own_cot = lax.dot_general(up_own[...], vcot[...], NT, preferred_element_type=F32)
+    own_cot = cot_dot(up_own[...], tail_own[...])
     for chip_n in range(CHIPS):
         for core_n in range(CORES):
             at = (chip_n * CORES + core_n) * (rank // GROUP)
@@ -242,12 +333,13 @@
     own_core = send(own_f32.at[1 - core], own_core_in, sibling)
     chip_moves[0] = scatter_chips(0, core_moves[0])
 
-    near(down_moves[2])
-    down_moves.append(relay(down_own, down_all, 3))
+    down.step3(True)
+    up.wrap1()
+    tail.wrap1()
     core_moves[1] = val_step(1)
-
-    near(up_moves[0])
-    up_moves.append(relay(up_own, up_all, 1))
+    down.step4()
+    up.step2()
+    tail.step2()
 
     own_core.wait_recv()
     own_sum = own_f32[core] + own_core_in[...]
@@ -259,21 +351,28 @@
     ]
     chip_moves[1] = scatter_chips(1, core_moves[1])
     core_moves[4] = cot_step(0)
+    down.relay1()
+    up.wrap2()
+    tail.wrap2()
+    chip_moves[4] = scatter_chips(4, core_moves[4])
+    up.step3(False)
+    tail.step3(True)
+    core_moves[5] = cot_step(1)
+    down.wait(10, 11)
     core_moves[2] = val_step(2)
-    chip_moves[4] = scatter_chips(4, core_moves[4])
+    down.relay2()
+    up.step4()
+    tail.step4()
+    chip_moves[5] = scatter_chips(5, core_moves[5])
     chip_moves[2] = scatter_chips(2, core_moves[2])
-
-    near(up_moves[1])
-    up_moves.append(relay(up_own, up_all, 2))
-    near(down_moves[3])
+    down.wait(13)
     core_moves[3] = val_step(3)
-    core_moves[5] = cot_step(1)
+    up.wait(10, 11)
+    tail.wait(10, 11)
+    core_moves[6] = cot_step(2)
+    up.relay1()
+    tail.relay1()
     chip_moves[3] = scatter_chips(3, core_moves[3])
-    chip_moves[5] = scatter_chips(5, core_moves[5])
-
-    near(up_moves[2])
-    up_moves.append(relay(up_own, up_all, 3))
-    core_moves[6] = cot_step(2)
     chip_moves[6] = scatter_chips(6, core_moves[6])
 
     def change(step):
@@ -290,7 +389,10 @@
     changes = [change(0), change(1)]
     own_change = jnp.sum(own_piece[0:8] * own_piece[8:16], axis=0, keepdims=True)
 
-    near(up_moves[3])
+    up.relay2()
+    tail.relay2()
+    up.wait(13)
+    tail.wait(13)
     core_moves[7] = cot_step(3)
     chip_moves[7] = scatter_chips(7, core_moves[7])
     changes.append(change(2))
@@ -306,17 +408,30 @@
 
     row = lax.broadcasted_iota(jnp.int32, (8, 128), 0)
     column = lax.broadcasted_iota(jnp.int32, (8, 128), 1)
-    from_behind = chip == 0
-    from_ahead = chip == 1
-    from_far_ahead = chip == 2
-    place = jnp.where(
-        from_behind,
-        reach - 1 - row,
-        jnp.where(
-            from_ahead, reach + 1 + row, jnp.where(from_far_ahead, 2 * reach - row, row)
-        ),
+    def ring_column(d):
+        return jnp.where(depth >= d, reach - d, 2 * reach - d)
+
+    def far_column(p):
+        return jnp.where(depth >= p, 2 * reach - p, reach - p)
+
+    def pick(p, q):
+        return jnp.where(low_half, far_column(p), far_column(q))
+
+    held_columns = (
+        (ring_column(1), ring_column(7), far_column(0), far_column(8)),
+        (ring_column(2), ring_column(6), far_column(1), far_column(7)),
+        (ring_column(3), ring_column(5), pick(6, 2), pick(5, 3)),
+        (ring_column(4), pick(2, 6), pick(3, 5), far_column(4)),
     )
-    place = jnp.where(row == STEPS, reach, place)
+    place = jnp.full((8, 128), reach, jnp.int32)
+    for unit in range(STEPS):
+        first, second, third, fourth = held_columns[unit]
+        mine = jnp.where(
+            chip == 0,
+            first,
+            jnp.where(chip == 1, second, jnp.where(chip == 2, third, fourth)),
+        )
+        place = jnp.where(row == unit, mine, place)
     chosen = (place == column) & (row <= STEPS)
     own_row = jnp.sum(jnp.where(chosen, own_part, 0.0), axis=0, keepdims=True)
     other_row = jnp.sum(jnp.where(chosen, other_part, 0.0), axis=0, keepdims=True)
@@ -336,6 +451,8 @@
     other_out[...] = result[1:2, :columns] / other_count
     for copy in started:
         copy.wait_send()
+    for when, copy in started_if:
+        pl.when(when)(copy.wait_send)
 
 
 def on_device(
@@ -355,8 +472,9 @@
     rows = validation_inputs.shape[1]
     rank = adapter_down_init.shape[2]
     piece = rank // CORES
+    split = (hidden // 256 + 1) * 128
     units = 2 * STEPS
-    copies = 2 * 4 * STEPS + 3 * (GROUP - 1) + units * CHIPS + CHIPS
+    copies = 3 * 22 + 3 * (GROUP - 1) + units * CHIPS + CHIPS
     any_spec = pl.BlockSpec(memory_space=pl.ANY)
     vmem_spec = pl.BlockSpec(memory_space=pltpu.VMEM)
     return pl.pallas_call(
@@ -372,11 +490,12 @@
             pltpu.VMEM((train, hidden), BF16),
             pltpu.VMEM((rows, width), BF16),
             pltpu.VMEM((rows, hidden), BF16),
-            pltpu.VMEM((width, rank), BF16),
             pltpu.VMEM((rank, width), BF16),
-            pltpu.VMEM((STEPS, 4 * rank, width), BF16),
-            pltpu.VMEM((rank, hidden), BF16),
-            pltpu.VMEM((STEPS, 4 * rank, hidden), BF16),
+            pltpu.VMEM((BLOCKS, rank, width), BF16),
+            pltpu.VMEM((rank, split), BF16),
+            pltpu.VMEM((BLOCKS, rank, split), BF16),
+            pltpu.VMEM((rank, hidden - split), BF16),
+            pltpu.VMEM((BLOCKS, rank, hidden - split), BF16),
             pltpu.VMEM((GROUP, rank // GROUP, train), F32),
             pltpu.VMEM((GROUP - 1, rank // GROUP, train), F32),
             pltpu.VMEM((rank // GROUP, train), F32),
@@ -396,9 +515,10 @@
             pltpu.SemaphoreType.DMA((5,)),
             pltpu.SemaphoreType.DMA((copies,)),
             pltpu.SemaphoreType.DMA((copies,)),
+            pltpu.SemaphoreType.DMA((3 * BLOCKS,)),
         ],
         compiler_params=pltpu.CompilerParams(
-            collective_id=0, has_side_effects=True, vmem_limit_bytes=48 * 1024 * 1024
+            collective_id=0, has_side_effects=True, vmem_limit_bytes=60 * 1024 * 1024
         ),
     )(
         stored_inputs[0],
@@ -407,7 +527,7 @@
         validation_inputs[0],
         validation_output_gradient[0],
         validation_row_skill,
-        adapter_down_init[0],
+        jnp.swapaxes(adapter_down_init[0], 0, 1),
     )
 
 

time: 131 us -> 106 us (0.81)
  Pallas kernels: 122 us -> 102 us
  local copies, waits for them, and re-layouts: 8.46 us -> 2.25 us
    pallas_call x1, Pallas kernels: 122 us -> 102 us  [on_device(): pl.pallas_call(functools.partial(kernel, skills, reach), out_shape=(jax.S...]
    unnamed x15 -> x2, local copies, waits for them, and re-layouts: 8.46 us -> 2.25 us
where the time goes in v2:
time: 106 us; the launch traced here: 105 us
  Pallas kernels  102 us (96%)
  local copies, waits for them, and re-layouts  2.25 us (2%)
    pallas_call x1, Pallas kernels, on_device(): pl.pallas_call(functools.partial(kernel, skills, reach), out_shape=(jax.S...  102 us
    unnamed x2, local copies, waits for them, and re-layouts  2.25 us

profile of v2, /device:TPU:7, one launch (start us, length us, event | category | flops | bytes accessed | tf_op | source)
XLA Modules:
  0.0 104.8 jit_solution(303180304645033458)
XLA Ops:
  0.6 101.9 %shard_map.86 = (f32[1,17]{1,0:T(1,128)}, f32[1,17]{1,0:T(1,128)}) custom-call(bf16[256,1024]{1,0:T(8,128)(2,1)} %bitcast.10, bf16[256,1920]{1,0:T(8,128)(2,1)} %bitcast.9, s32[1,256]{1,0:T(1,128)} %index_ref.1, bf16[512,1024]{1,0:T(8,128)(2,1)} %bitcast.8, bf16[512,1920]{1,0:T(8,128)(2,1)} %bitcast.7, s32[1,512]{1,0:T(1,128)} %label_ref.1, ...), custom_call_target="tpu_custom_call" | custom-call | tf_op jit(solution)/shard_map/pallas_call | solution.py:480
  102.6 1.1 %copy.11 = f32[1,17]{1,0:T(1,128)} copy(f32[1,17]{1,0:T(1,128)} %get-tuple-element.4) | data formatting | bytes 136
  103.7 1.1 %copy.12 = f32[1,17]{1,0:T(1,128)} copy(f32[1,17]{1,0:T(1,128)} %get-tuple-element.5) | data formatting | bytes 136

commit v3 on v2

v3 whole, which is shorter than its diff:
```python
import functools

import jax
import jax.numpy as jnp
from jax import lax
from jax.experimental import pallas as pl
from jax.experimental.pallas import tpu as pltpu
from jax.sharding import PartitionSpec as P

F32 = jnp.float32
BF16 = jnp.bfloat16
STEPS = 4
BLOCKS = 17
PIECES = 2
CHIPS = 4
CORES = 2
GROUP = 8
LINE = 4
PASSING = 16
NT = (((1,), (1,)), ((), ()))


def kernel(
    skills,
    reach,
    act_hbm,
    cot_hbm,
    index_ref,
    vact_hbm,
    vcot_hbm,
    label_ref,
    down_hbm,
    own_out,
    other_out,
    act,
    cot,
    vact,
    vcot,
    down_own,
    down_all,
    up_own0,
    up_all0,
    up_own1,
    up_all1,
    part,
    part_in,
    share,
    full,
    unit_halves,
    unit_core_in,
    unit_out,
    unit_chip_in,
    unit_full,
    own_halves,
    own_core_in,
    own_out_f32,
    own_chip_in,
    own_full,
    table,
    table_in,
    load_sem,
    send_sem,
    recv_sem,
    block_sem,
):
    unit_refs = (unit_halves, unit_core_in, unit_out, unit_chip_in, unit_full)
    own_refs = (own_halves, own_core_in, own_out_f32, own_chip_in, own_full)
    me = lax.axis_index("skill")
    lane_pos = lax.axis_index("tensor")
    chip = lane_pos // CORES
    core = lax.rem(lane_pos, CORES)
    rank = down_own.shape[0]
    train = act.shape[0]
    piece = rank // CORES

    loads = []
    for n, (src, dst) in enumerate(
        [(down_hbm, down_own), (act_hbm, act), (vact_hbm, vact), (cot_hbm, cot), (vcot_hbm, vcot)]
    ):
        copy = pltpu.make_async_copy(src, dst, load_sem.at[n])
        copy.start()
        loads.append(copy)
    load_down, load_act, load_vact, load_cot, load_vcot = loads

    def skill_at(shift):
        return (lax.rem(me + shift + skills, skills), lane_pos)

    def tensor_at(shift):
        return (me, lax.rem(lane_pos + shift, GROUP))

    def chip_at(shift):
        return (me, lax.rem(chip + shift, CHIPS) * CORES + core)

    sibling = (me, chip * CORES + (1 - core))

    barrier = pltpu.get_barrier_semaphore()
    depth = lax.rem(me, reach)
    half = reach // 2
    low_half = depth < half
    line = lax.rem(me // reach, LINE)
    first_in_line = line == 0
    last_in_line = line == LINE - 1

    def ring_at(shift):
        return (me - depth + lax.rem(depth + shift + reach, reach), lane_pos)

    partners = [ring_at(1), ring_at(-1), skill_at(reach), skill_at(-reach)]
    partners += [tensor_at(d) for d in range(1, GROUP)]
    for partner in partners:
        pl.semaphore_signal(
            barrier, inc=1, device_id=partner, device_id_type=pl.DeviceIdType.MESH
        )

    started = []
    started_if = []

    def send(src, dst, target):
        n = len(started) + len(started_if)
        copy = pltpu.make_async_remote_copy(
            src_ref=src,
            dst_ref=dst,
            send_sem=send_sem.at[n],
            recv_sem=recv_sem.at[n],
            device_id=target,
            device_id_type=pl.DeviceIdType.MESH,
        )
        copy.start()
        started.append(copy)
        return copy

    class Stream:
        def __init__(self, own, held):
            self.own, self.held = own, held
            self.base = len(streams) * BLOCKS
            streams.append(self)

        def block(self, slot):
            return self.own if slot is None else self.held.at[slot]

        def send(self, source, slot, target, when=None):
            n = len(started) + len(started_if)
            copy = pltpu.make_async_remote_copy(
                src_ref=self.block(source),
                dst_ref=self.held.at[slot],
                send_sem=send_sem.at[n],
                recv_sem=block_sem.at[self.base + slot],
                device_id=target,
                device_id_type=pl.DeviceIdType.MESH,
            )
            if when is None:
                copy.start()
                started.append(copy)
            else:
                pl.when(when)(copy.start)
                started_if.append((when, copy))

        def wait(self, *slots):
            for slot in slots:
                pltpu.make_async_remote_copy(
                    src_ref=self.own,
                    dst_ref=self.held.at[slot],
                    send_sem=send_sem.at[0],
                    recv_sem=block_sem.at[self.base + slot],
                    device_id=sibling,
                    device_id_type=pl.DeviceIdType.MESH,
                ).wait_recv()

        def step0(self):
            self.send(None, 0, ring_at(1))
            self.send(None, 1, ring_at(-1))
            self.send(None, 2, skill_at(-reach))
            self.send(None, 3, skill_at(reach))

        def step1(self):
            self.wait(0, 1)
            self.send(0, 4, ring_at(1))
            self.send(1, 5, ring_at(-1))
            self.send(0, 6, skill_at(-reach), depth >= 1)
            self.send(1, 7, skill_at(reach), depth <= reach - 2)

        def step2(self):
            self.wait(4, 5)
            self.send(4, 8, ring_at(1))
            self.send(5, 9, ring_at(-1))
            self.send(
                4, 10, skill_at(jnp.where(depth >= 2, -reach, reach)), (depth >= 2) | ~last_in_line
            )
            self.send(
                5, 11, skill_at(jnp.where(depth <= reach - 3, reach, -reach)), (depth <= reach - 3) | ~first_in_line
            )

        def wrap(self):
            self.wait(2, 3)
            self.send(3, 6, ring_at(1), depth == reach - 1)
            self.send(2, 7, ring_at(-1), depth == 0)
            self.send(
                jnp.where(low_half, 2, 3),
                PASSING,
                ring_at(jnp.where(low_half, -1, 1)),
                (first_in_line & (depth == reach - 2)) | (last_in_line & (depth == 1)),
            )

        def wrap2(self):
            passing = (first_in_line & (depth == reach - 1)) | (last_in_line & (depth == 0))
            pl.when(passing)(lambda: self.wait(PASSING))
            self.send(
                PASSING,
                jnp.where(low_half, 11, 10),
                ring_at(jnp.where(low_half, -1, 1)),
                passing,
            )
            self.wait(6, 7)
            self.send(
                jnp.where(low_half, 6, 7),
                jnp.where(low_half, 10, 11),
                ring_at(jnp.where(low_half, 1, -1)),
                (first_in_line & (depth == 0)) | (last_in_line & (depth == reach - 1)),
            )
        def relay2(self):
            self.wait(10, 11)
            self.send(11, 14, ring_at(-1), (depth >= 1) & (depth <= half))
            self.send(10, 13, ring_at(1), (depth >= half - 1) & (depth <= reach - 2))

        def step3(self):
            self.wait(8, 9)
            self.send(8, 12, ring_at(1), lax.rem(depth + 1, reach) < half)
            self.send(9, 12, ring_at(-1), lax.rem(depth + reach - 1, reach) >= half)
            self.send(
                8,
                13,
                skill_at(jnp.where(depth == half - 1, -reach, reach)),
                low_half,
            )
            self.send(
                9,
                14,
                skill_at(jnp.where(depth == half, reach, -reach)),
                ~low_half,
            )

        def relay3(self):
            near_slot = jnp.where(low_half, 14, 13)
            self.wait(near_slot)
            self.send(
                near_slot,
                15,
                ring_at(jnp.where(low_half, -1, 1)),
                (depth >= 1) & (depth <= reach - 2),
            )
            middle = (depth == half) | (depth == half - 1)
            pl.when(middle)(lambda: self.wait(jnp.where(low_half, 13, 14)))
            self.send(
                jnp.where(low_half, 13, 14), 15, ring_at(jnp.where(low_half, 1, -1)), middle
            )

        def last(self):
            self.wait(12, 15)
            pl.when((depth < half - 1) | (depth > half))(
                lambda: self.wait(jnp.where(low_half, 13, 14))
            )

    streams = []

    class Projection:
        def __init__(self, refs, index):
            self.halves, self.core_in, self.out, self.chip_in, self.full = [
                ref.at[index] for ref in refs
            ]

        def to_core(self, product):
            parts = product.reshape(CHIPS, CORES, -1, product.shape[1])
            for c in range(CORES):
                self.halves[c] = parts[:, c]
            self.move = send(self.halves.at[1 - core], self.core_in, sibling)

        def to_owners(self):
            self.move.wait_recv()
            both = self.halves[core] + self.core_in[...]
            self.out[...] = both.astype(self.out.dtype)
            self.core_in[...] = both
            self.moves = [
                send(
                    self.out.at[lax.rem(chip + d, CHIPS)], self.chip_in.at[d - 1], chip_at(d)
                )
                for d in range(1, CHIPS)
            ]

        def to_chips(self):
            value = self.core_in[chip]
            for d in range(CHIPS - 1):
                self.moves[d].wait_recv()
                value = value + self.chip_in[d].astype(F32)
            mine = self.full.at[core, chip]
            mine[...] = value.astype(self.full.dtype)
            self.moves = [send(mine, mine, chip_at(d)) for d in range(1, CHIPS)]

        def to_sibling(self):
            for move in self.moves:
                move.wait_recv()
            self.move = send(self.full.at[core], self.full.at[core], sibling)

        def change(self, product):
            self.move.wait_recv()
            parts = product.reshape(CHIPS, CORES, -1, product.shape[1])
            sums = []
            for c in range(CORES):
                sums.append(jnp.sum(parts[:, c] * self.full[c].astype(F32), axis=1))
            return sums[0] + sums[1]

    load_down.wait()
    load_act.wait()
    part[...] = lax.dot_general(
        down_own[...], act[...], NT, preferred_element_type=F32
    ).reshape(part.shape)
    pl.semaphore_wait(barrier, len(partners))
    down = Stream(down_own, down_all)
    ups = [Stream(*refs) for refs in ((up_own0, up_all0), (up_own1, up_all1))]
    edges = [0]
    for up in ups:
        edges.append(edges[-1] + up.own.shape[1])
    down.step0()

    part_moves = [
        send(part.at[lax.rem(lane_pos + d, GROUP)], part_in.at[d - 1], tensor_at(d))
        for d in range(1, GROUP)
    ]
    load_vact.wait()
    own = Projection(own_refs, 0)
    units = [Projection(unit_refs, n) for n in range(STEPS)]
    own.to_core(lax.dot_general(down_own[...], vact[...], NT, preferred_element_type=F32))
    for copy in part_moves:
        copy.wait_recv()
    summed = part[lane_pos]
    for d in range(GROUP - 1):
        summed = summed + part_in[d]
    share[...] = summed
    full[lane_pos] = summed
    full_moves = [send(share, full.at[lane_pos], tensor_at(d)) for d in range(1, GROUP)]

    down.step1()
    own.to_owners()

    stored = lax.broadcasted_iota(jnp.int32, (train, train), 0)
    hits = jnp.where(stored == index_ref[...], 1.0, 0.0).astype(BF16)
    counts = lax.dot_general(
        jnp.ones((8, train), BF16), hits, NT, preferred_element_type=F32
    )[0:1]

    load_cot.wait()
    for copy in full_moves:
        copy.wait_recv()
    proj = full[...].reshape(rank, train).astype(BF16).astype(F32)
    weighted = proj * counts
    high = weighted.astype(BF16)
    low = (weighted - high.astype(F32)).astype(BF16)
    product = jnp.dot(
        jnp.concatenate([high, low], axis=0), cot[...], preferred_element_type=F32
    )
    factor = ((product[:rank] + product[rank:]) * (-1.0 / train)).astype(BF16)
    for n, up in enumerate(ups):
        up.own[...] = factor[:, edges[n] : edges[n + 1]]
        up.step0()
    down.step2()
    down.wrap()

    def val_step(unit):
        rows = down_all[4 * unit : 4 * unit + 4].reshape(4 * rank, down_own.shape[1])
        units[unit].to_core(
            lax.dot_general(rows, vact[...], NT, preferred_element_type=F32)
        )

    def cot_dot(blocks):
        result = 0.0
        for n, rows in enumerate(blocks):
            result = result + lax.dot_general(
                rows, vcot[:, edges[n] : edges[n + 1]], NT, preferred_element_type=F32
            )
        return result

    def cot_step(unit):
        blocks = [
            up.held[4 * unit : 4 * unit + 4].reshape(4 * rank, up.own.shape[1]) for up in ups
        ]
        return units[unit].change(cot_dot(blocks))

    val_step(0)
    own.to_chips()
    down.step3()
    units[0].to_owners()
    for up in ups:
        up.step1()
    down.wrap2()
    val_step(1)
    units[0].to_chips()
    down.relay2()
    units[1].to_owners()
    for up in ups:
        up.step2()
    own.to_sibling()
    val_step(2)
    units[0].to_sibling()
    down.relay3()
    for up in ups:
        up.wrap()
    units[1].to_chips()
    units[2].to_owners()
    down.last()
    val_step(3)
    for up in ups:
        up.step3()
    load_vcot.wait()
    own_product = cot_dot([up.own[...] for up in ups])
    own_change = own.change(own_product)
    own_change = jnp.sum(own_change, axis=0, keepdims=True)
    units[3].to_owners()
    units[2].to_chips()
    units[1].to_sibling()
    for up in ups:
        up.wrap2()
    changes = [cot_step(0)]
    for up in ups:
        up.relay2()
    units[3].to_chips()
    units[2].to_sibling()
    changes.append(cot_step(1))
    for up in ups:
        up.relay3()
    units[3].to_sibling()
    changes.append(cot_step(2))
    for up in ups:
        up.last()
    changes.append(cot_step(3))

    own_mask = (label_ref[...] == me).astype(F32)
    other_mask = 1.0 - own_mask
    stack = jnp.concatenate(
        changes + [own_change, jnp.zeros((7, own_change.shape[1]), F32)], axis=0
    )
    own_part = jnp.sum(stack * own_mask, axis=1, keepdims=True)
    other_part = jnp.sum(stack * other_mask, axis=1, keepdims=True)

    row = lax.broadcasted_iota(jnp.int32, (24, 128), 0)
    column = lax.broadcasted_iota(jnp.int32, (24, 128), 1)

    def ring_column(d):
        return jnp.where(depth >= d, reach - d, 2 * reach - d)

    def far_column(p):
        return jnp.where(depth >= p, 2 * reach - p, reach - p)

    held_columns = (
        (ring_column(1), ring_column(7), far_column(0), far_column(8)),
        (ring_column(2), ring_column(6), far_column(1), far_column(7)),
        (ring_column(3), ring_column(5), far_column(2), far_column(6)),
        (ring_column(4), far_column(3), far_column(5), far_column(4)),
    )
    place = jnp.where(row == 4 * STEPS, reach, -1)
    for unit in range(STEPS):
        for n in range(4):
            place = jnp.where(row == 4 * unit + n, held_columns[unit][n], place)
    chosen = place == column
    own_row = jnp.sum(jnp.where(chosen, own_part, 0.0), axis=0, keepdims=True)
    other_row = jnp.sum(jnp.where(chosen, other_part, 0.0), axis=0, keepdims=True)
    top = row[:8]
    table[...] = jnp.where(top == 0, own_row, jnp.where(top == 1, other_row, 0.0))
    table_moves = [send(table, table_in.at[d - 1], tensor_at(d)) for d in range(1, GROUP)]
    own_count = jnp.maximum(jnp.sum(own_mask, axis=1, keepdims=True), 1.0)
    other_count = jnp.maximum(jnp.sum(other_mask, axis=1, keepdims=True), 1.0)
    for copy in table_moves:
        copy.wait_recv()
    result = jnp.zeros((8, 128), F32)
    for t in range(GROUP):
        away = lax.rem(lane_pos - t + GROUP, GROUP)
        theirs = table_in[lax.max(away - 1, 0)]
        result = result + jnp.where(away == 0, table[...], theirs)
    columns = own_out.shape[1]
    own_out[...] = result[0:1, :columns] / own_count
    other_out[...] = result[1:2, :columns] / other_count
    for copy in started:
        copy.wait_send()
    for when, copy in started_if:
        pl.when(when)(copy.wait_send)


def on_device(
    stored_inputs,
    stored_output_gradient,
    training_token_index,
    validation_inputs,
    validation_output_gradient,
    validation_row_skill,
    adapter_down_init,
):
    skills = lax.axis_size("skill")
    reach = skills // 8
    columns = 2 * reach + 1
    _, train, width = stored_inputs.shape
    hidden = stored_output_gradient.shape[2]
    rows = validation_inputs.shape[1]
    rank = adapter_down_init.shape[2]
    piece = rank // CORES
    cuts = [hidden // 128 * n // PIECES * 128 for n in range(PIECES + 1)]
    splits = [cuts[n + 1] - cuts[n] for n in range(PIECES)]
    share = rank // GROUP
    copies = (1 + PIECES) * 28 + 3 * (GROUP - 1) + (STEPS + 1) * 2 * CHIPS
    any_spec = pl.BlockSpec(memory_space=pl.ANY)
    vmem_spec = pl.BlockSpec(memory_space=pltpu.VMEM)
    return pl.pallas_call(
        functools.partial(kernel, skills, reach),
        out_shape=(
            jax.ShapeDtypeStruct((1, columns), F32),
            jax.ShapeDtypeStruct((1, columns), F32),
        ),
        in_specs=[any_spec, any_spec, vmem_spec, any_spec, any_spec, vmem_spec, any_spec],
        out_specs=(vmem_spec, vmem_spec),
        scratch_shapes=[
            pltpu.VMEM((train, width), BF16),
            pltpu.VMEM((train, hidden), BF16),
            pltpu.VMEM((rows, width), BF16),
            pltpu.VMEM((rows, hidden), BF16),
            pltpu.VMEM((rank, width), BF16),
            pltpu.VMEM((BLOCKS, rank, width), BF16),
            *[
                pltpu.VMEM(shape, BF16)
                for width_n in splits
                for shape in ((rank, width_n), (BLOCKS, rank, width_n))
            ],
            pltpu.VMEM((GROUP, rank // GROUP, train), F32),
            pltpu.VMEM((GROUP - 1, rank // GROUP, train), F32),
            pltpu.VMEM((rank // GROUP, train), F32),
            pltpu.VMEM((GROUP, rank // GROUP, train), F32),
            pltpu.VMEM((STEPS, CORES, CHIPS, piece, rows), F32),
            pltpu.VMEM((STEPS, CHIPS, piece, rows), F32),
            pltpu.VMEM((STEPS, CHIPS, piece, rows), BF16),
            pltpu.VMEM((STEPS, CHIPS - 1, piece, rows), BF16),
            pltpu.VMEM((STEPS, CORES, CHIPS, piece, rows), BF16),
            pltpu.VMEM((1, CORES, CHIPS, share, rows), F32),
            pltpu.VMEM((1, CHIPS, share, rows), F32),
            pltpu.VMEM((1, CHIPS, share, rows), F32),
            pltpu.VMEM((1, CHIPS - 1, share, rows), F32),
            pltpu.VMEM((1, CORES, CHIPS, share, rows), F32),
            pltpu.VMEM((8, 128), F32),
            pltpu.VMEM((GROUP - 1, 8, 128), F32),
            pltpu.SemaphoreType.DMA((5,)),
            pltpu.SemaphoreType.DMA((copies,)),
            pltpu.SemaphoreType.DMA((copies,)),
            pltpu.SemaphoreType.DMA(((1 + PIECES) * BLOCKS,)),
        ],
        compiler_params=pltpu.CompilerParams(
            collective_id=0, has_side_effects=True, vmem_limit_bytes=60 * 1024 * 1024
        ),
    )(
        stored_inputs[0],
        stored_output_gradient[0],
        training_token_index,
        validation_inputs[0],
        validation_output_gradient[0],
        validation_row_skill,
        jnp.swapaxes(adapter_down_init[0], 0, 1),
    )


def solution(mesh):
    in_specs = (
        P("skill", None, "tensor"),
        P("skill", None, "tensor"),
        P("skill", None),
        P("skill", None, "tensor"),
        P("skill", None, "tensor"),
        P("skill", None),
        P("skill", "tensor", None),
    )
    out_specs = (P("skill", None), P("skill", None))
    return jax.shard_map(
        on_device, mesh=mesh, in_specs=in_specs, out_specs=out_specs, check_vma=False
    )
```

time: 106 us -> 97.2 us (0.917); the launches traced: 105 us -> 97.1 us
  Pallas kernels: 102 us -> 94.2 us
    pallas_call x1, Pallas kernels: 102 us -> 94.2 us  [on_device(): pl.pallas_call(functools.partial(kernel, skills, reach), out_shape=(jax.S...]
where the time goes in v3:
time: 97.2 us; the launch traced here: 97.1 us
  Pallas kernels  94.2 us (97%)
  local copies, waits for them, and re-layouts  2.25 us (2%)
    pallas_call x1, Pallas kernels, on_device(): pl.pallas_call(functools.partial(kernel, skills, reach), out_shape=(jax.S...  94.2 us
    unnamed x2, local copies, waits for them, and re-layouts  2.25 us

profile of v3, /device:TPU:7, one launch (start us, length us, event | category | flops | bytes accessed | tf_op | source)
XLA Modules:
  0.0 97.1 jit_solution(11678293458448862585)
XLA Ops:
  0.6 94.2 %shard_map.86 = (f32[1,17]{1,0:T(1,128)}, f32[1,17]{1,0:T(1,128)}) custom-call(bf16[256,1024]{1,0:T(8,128)(2,1)} %bitcast.10, bf16[256,1920]{1,0:T(8,128)(2,1)} %bitcast.9, s32[1,256]{1,0:T(1,128)} %index_ref.1, bf16[512,1024]{1,0:T(8,128)(2,1)} %bitcast.8, bf16[512,1920]{1,0:T(8,128)(2,1)} %bitcast.7, s32[1,512]{1,0:T(1,128)} %label_ref.1, ...), custom_call_target="tpu_custom_call" | custom-call | tf_op jit(solution)/shard_map/pallas_call | solution.py:508
  94.8 1.1 %copy.11 = f32[1,17]{1,0:T(1,128)} copy(f32[1,17]{1,0:T(1,128)} %get-tuple-element.4) | data formatting | bytes 136
  95.9 1.1 %copy.12 = f32[1,17]{1,0:T(1,128)} copy(f32[1,17]{1,0:T(1,128)} %get-tuple-element.5) | data formatting | bytes 136

commit v4 on v3

--- a/solution.py
+++ b/solution.py
@@ -30,8 +30,7 @@
     vcot_hbm,
     label_ref,
     down_hbm,
-    own_out,
-    other_out,
+    deltas_out,
     act,
     cot,
     vact,
@@ -100,6 +99,13 @@
     line = lax.rem(me // reach, LINE)
     first_in_line = line == 0
     last_in_line = line == LINE - 1
+    edge = (depth <= 1) | (depth >= reach - 2)
+    middle = (depth == half) | (depth == half - 1)
+    turning = (first_in_line & (depth == 0)) | (last_in_line & (depth == reach - 1))
+    stepping = (first_in_line & (depth >= 1) & (depth <= half)) | (
+        last_in_line & (depth >= half - 1) & (depth <= reach - 2)
+    )
+    onward = turning | stepping
 
     def ring_at(shift):
         return (me - depth + lax.rem(depth + shift + reach, reach), lane_pos)
@@ -183,14 +189,29 @@
             self.send(4, 8, ring_at(1))
             self.send(5, 9, ring_at(-1))
             self.send(
-                4, 10, skill_at(jnp.where(depth >= 2, -reach, reach)), (depth >= 2) | ~last_in_line
-            )
-            self.send(
-                5, 11, skill_at(jnp.where(depth <= reach - 3, reach, -reach)), (depth <= reach - 3) | ~first_in_line
-            )
+                4,
+                10,
+                skill_at(jnp.where(depth >= 2, -reach, reach)),
+                jnp.where(depth >= 2, low_half | ~first_in_line, ~last_in_line),
+            )
+            self.send(
+                5,
+                11,
+                skill_at(jnp.where(depth <= reach - 3, reach, -reach)),
+                jnp.where(depth <= reach - 3, ~low_half | ~last_in_line, ~first_in_line),
+            )
+
+        def settle1(self):
+            pl.when(~edge)(lambda: self.wait(2, 3))
+
+        def settle2(self):
+            pl.when(~onward)(lambda: self.wait(6, 7))
+
+        def settle3(self):
+            pl.when(~middle)(lambda: self.wait(jnp.where(low_half, 10, 11)))
 
         def wrap(self):
-            self.wait(2, 3)
+            pl.when(edge)(lambda: self.wait(2, 3))
             self.send(3, 6, ring_at(1), depth == reach - 1)
             self.send(2, 7, ring_at(-1), depth == 0)
             self.send(
@@ -209,17 +230,35 @@
                 ring_at(jnp.where(low_half, -1, 1)),
                 passing,
             )
-            self.wait(6, 7)
+            pl.when(onward)(lambda: self.wait(6, 7))
             self.send(
                 jnp.where(low_half, 6, 7),
                 jnp.where(low_half, 10, 11),
                 ring_at(jnp.where(low_half, 1, -1)),
-                (first_in_line & (depth == 0)) | (last_in_line & (depth == reach - 1)),
+                turning,
+            )
+            self.send(
+                jnp.where(first_in_line, 7, 6),
+                jnp.where(first_in_line, 11, 10),
+                ring_at(jnp.where(first_in_line, -1, 1)),
+                stepping,
             )
         def relay2(self):
-            self.wait(10, 11)
-            self.send(11, 14, ring_at(-1), (depth >= 1) & (depth <= half))
-            self.send(10, 13, ring_at(1), (depth >= half - 1) & (depth <= reach - 2))
+            near_slot, far_slot = jnp.where(low_half, 11, 10), jnp.where(low_half, 10, 11)
+            self.wait(near_slot)
+            self.send(
+                near_slot,
+                jnp.where(low_half, 14, 13),
+                ring_at(jnp.where(low_half, -1, 1)),
+                (depth >= 1) & (depth <= reach - 2),
+            )
+            pl.when(middle)(lambda: self.wait(far_slot))
+            self.send(
+                far_slot,
+                jnp.where(low_half, 13, 14),
+                ring_at(jnp.where(low_half, 1, -1)),
+                middle,
+            )
 
         def step3(self):
             self.wait(8, 9)
@@ -247,7 +286,6 @@
                 ring_at(jnp.where(low_half, -1, 1)),
                 (depth >= 1) & (depth <= reach - 2),
             )
-            middle = (depth == half) | (depth == half - 1)
             pl.when(middle)(lambda: self.wait(jnp.where(low_half, 13, 14)))
             self.send(
                 jnp.where(low_half, 13, 14), 15, ring_at(jnp.where(low_half, 1, -1)), middle
@@ -338,6 +376,7 @@
     full_moves = [send(share, full.at[lane_pos], tensor_at(d)) for d in range(1, GROUP)]
 
     down.step1()
+    down.wrap()
     own.to_owners()
 
     stored = lax.broadcasted_iota(jnp.int32, (train, train), 0)
@@ -361,7 +400,8 @@
         up.own[...] = factor[:, edges[n] : edges[n + 1]]
         up.step0()
     down.step2()
-    down.wrap()
+    down.wrap2()
+    down.settle1()
 
     def val_step(unit):
         rows = down_all[4 * unit : 4 * unit + 4].reshape(4 * rank, down_own.shape[1])
@@ -389,43 +429,50 @@
     units[0].to_owners()
     for up in ups:
         up.step1()
-    down.wrap2()
+    down.relay2()
+    for up in ups:
+        up.wrap()
+    down.settle2()
     val_step(1)
     units[0].to_chips()
-    down.relay2()
     units[1].to_owners()
     for up in ups:
         up.step2()
+    for up in ups:
+        up.wrap2()
+    down.relay3()
     own.to_sibling()
+    down.settle3()
     val_step(2)
     units[0].to_sibling()
-    down.relay3()
-    for up in ups:
-        up.wrap()
     units[1].to_chips()
     units[2].to_owners()
+    for up in ups:
+        up.step3()
     down.last()
     val_step(3)
     for up in ups:
-        up.step3()
+        up.relay2()
+    units[3].to_owners()
+    units[2].to_chips()
+    units[1].to_sibling()
+    for up in ups:
+        up.relay3()
+    units[3].to_chips()
+    units[2].to_sibling()
     load_vcot.wait()
     own_product = cot_dot([up.own[...] for up in ups])
     own_change = own.change(own_product)
     own_change = jnp.sum(own_change, axis=0, keepdims=True)
-    units[3].to_owners()
-    units[2].to_chips()
-    units[1].to_sibling()
-    for up in ups:
-        up.wrap2()
+    for up in ups:
+        up.settle1()
     changes = [cot_step(0)]
     for up in ups:
-        up.relay2()
-    units[3].to_chips()
-    units[2].to_sibling()
+        up.settle2()
     changes.append(cot_step(1))
-    for up in ups:
-        up.relay3()
     units[3].to_sibling()
+    for up in ups:
+        up.settle3()
     changes.append(cot_step(2))
     for up in ups:
         up.last()
@@ -473,9 +520,9 @@
         away = lax.rem(lane_pos - t + GROUP, GROUP)
         theirs = table_in[lax.max(away - 1, 0)]
         result = result + jnp.where(away == 0, table[...], theirs)
-    columns = own_out.shape[1]
-    own_out[...] = result[0:1, :columns] / own_count
-    other_out[...] = result[1:2, :columns] / other_count
+    columns = deltas_out.shape[1]
+    deltas_out[0:1] = result[0:1, :columns] / own_count
+    deltas_out[1:2] = result[1:2, :columns] / other_count
     for copy in started:
         copy.wait_send()
     for when, copy in started_if:
@@ -505,14 +552,11 @@
     copies = (1 + PIECES) * 28 + 3 * (GROUP - 1) + (STEPS + 1) * 2 * CHIPS
     any_spec = pl.BlockSpec(memory_space=pl.ANY)
     vmem_spec = pl.BlockSpec(memory_space=pltpu.VMEM)
-    return pl.pallas_call(
+    deltas = pl.pallas_call(
         functools.partial(kernel, skills, reach),
-        out_shape=(
-            jax.ShapeDtypeStruct((1, columns), F32),
-            jax.ShapeDtypeStruct((1, columns), F32),
-        ),
+        out_shape=jax.ShapeDtypeStruct((2, columns), F32),
         in_specs=[any_spec, any_spec, vmem_spec, any_spec, any_spec, vmem_spec, any_spec],
-        out_specs=(vmem_spec, vmem_spec),
+        out_specs=vmem_spec,
         scratch_shapes=[
             pltpu.VMEM((train, width), BF16),
             pltpu.VMEM((train, hidden), BF16),
@@ -558,6 +602,7 @@
         validation_row_skill,
         jnp.swapaxes(adapter_down_init[0], 0, 1),
     )
+    return deltas[0:1], deltas[1:2]
 
 
 def solution(mesh):

time: 97.2 us -> 94.4 us (0.971)
  Pallas kernels: 94.2 us -> 92.4 us
  local copies, waits for them, and re-layouts: 2.25 us -> 1.25 us
    unnamed x2 -> x0, local copies, waits for them, and re-layouts: 2.25 us -> none
    pallas_call x1, Pallas kernels: 94.2 us -> 92.4 us  [on_device(): pl.pallas_call(functools.partial(kernel, skills, reach), out_shape=jax.Sh...]
    slice x0 -> x1, local copies, waits for them, and re-layouts: none -> 1.25 us  [on_device(): return (deltas[0:1], deltas[1:2])]
where the time goes in v4:
time: 94.4 us; the launch traced here: 94.3 us
  Pallas kernels  92.4 us (98%)
  local copies, waits for them, and re-layouts  1.25 us (1%)
    pallas_call x1, Pallas kernels, on_device(): pl.pallas_call(functools.partial(kernel, skills, reach), out_shape=jax.Sh...  92.4 us

profile of v4, /device:TPU:7, one launch (start us, length us, event | category | flops | bytes accessed | tf_op | source)
XLA Modules:
  0.0 94.3 jit_solution(9052023642885714500)
XLA Ops:
  0.6 92.4 %shard_map.86 = f32[2,17]{1,0:T(2,128)} custom-call(bf16[256,1024]{1,0:T(8,128)(2,1)} %bitcast.10, bf16[256,1920]{1,0:T(8,128)(2,1)} %bitcast.9, s32[1,256]{1,0:T(1,128)} %index_ref.1, bf16[512,1024]{1,0:T(8,128)(2,1)} %bitcast.8, bf16[512,1920]{1,0:T(8,128)(2,1)} %bitcast.7, s32[1,512]{1,0:T(1,128)} %label_ref.1, bf16[64,1024]{1,0:T(8,128)(2,1)} %bitcast.11), custom_call_target="tpu_custom_call" | custom-call | tf_op jit(solution)/shard_map/pallas_call | solution.py:555
  93.0 1.3 %fusion = (f32[1,17]{1,0:T(1,128)}, f32[1,17]{1,0:T(1,128)}) fusion(f32[2,17]{1,0:T(2,128)} %shard_map.86), kind=kLoop, calls=%fused_computation | loop fusion | bytes 272 | tf_op jit(solution)/shard_map/slice | solution.py:605

commit v5 on v4

--- a/solution.py
+++ b/solution.py
@@ -101,6 +101,11 @@
     last_in_line = line == LINE - 1
     edge = (depth <= 1) | (depth >= reach - 2)
     middle = (depth == half) | (depth == half - 1)
+    inner = (
+        middle
+        | (last_in_line & (depth == half - 2))
+        | (first_in_line & (depth == half + 1))
+    )
     turning = (first_in_line & (depth == 0)) | (last_in_line & (depth == reach - 1))
     stepping = (first_in_line & (depth >= 1) & (depth <= half)) | (
         last_in_line & (depth >= half - 1) & (depth <= reach - 2)
@@ -208,7 +213,7 @@
             pl.when(~onward)(lambda: self.wait(6, 7))
 
         def settle3(self):
-            pl.when(~middle)(lambda: self.wait(jnp.where(low_half, 10, 11)))
+            pl.when(~inner)(lambda: self.wait(jnp.where(low_half, 10, 11)))
 
         def wrap(self):
             pl.when(edge)(lambda: self.wait(2, 3))
@@ -252,12 +257,12 @@
                 ring_at(jnp.where(low_half, -1, 1)),
                 (depth >= 1) & (depth <= reach - 2),
             )
-            pl.when(middle)(lambda: self.wait(far_slot))
+            pl.when(inner)(lambda: self.wait(far_slot))
             self.send(
                 far_slot,
                 jnp.where(low_half, 13, 14),
                 ring_at(jnp.where(low_half, 1, -1)),
-                middle,
+                inner,
             )
 
         def step3(self):
@@ -268,13 +273,13 @@
                 8,
                 13,
                 skill_at(jnp.where(depth == half - 1, -reach, reach)),
-                low_half,
+                low_half & ((depth != half - 1) | ~first_in_line),
             )
             self.send(
                 9,
                 14,
                 skill_at(jnp.where(depth == half, reach, -reach)),
-                ~low_half,
+                ~low_half & ((depth != half) | ~last_in_line),
             )
 
         def relay3(self):
@@ -323,14 +328,25 @@
                 for d in range(1, CHIPS)
             ]
 
-        def to_chips(self):
+        def to_chips(self, direct=False):
             value = self.core_in[chip]
             for d in range(CHIPS - 1):
                 self.moves[d].wait_recv()
                 value = value + self.chip_in[d].astype(F32)
             mine = self.full.at[core, chip]
             mine[...] = value.astype(self.full.dtype)
-            self.moves = [send(mine, mine, chip_at(d)) for d in range(1, CHIPS)]
+            ways = (1, 2, 3) if direct else (1, 3)
+            self.moves = [send(mine, mine, chip_at(d)) for d in ways]
+
+        def to_far(self):
+            cut = self.full.shape[2] // 2
+            for n, (source, d) in enumerate(((3, 1), (1, 3))):
+                self.moves[n].wait_recv()
+                part = self.full.at[
+                    core, lax.rem(chip + source, CHIPS), pl.ds(n * cut, cut)
+                ]
+                self.moves.append(send(part, part, chip_at(d)))
+            self.moves = self.moves[2:]
 
         def to_sibling(self):
             for move in self.moves:
@@ -424,7 +440,7 @@
         return units[unit].change(cot_dot(blocks))
 
     val_step(0)
-    own.to_chips()
+    own.to_chips(True)
     down.step3()
     units[0].to_owners()
     for up in ups:
@@ -444,7 +460,7 @@
     own.to_sibling()
     down.settle3()
     val_step(2)
-    units[0].to_sibling()
+    units[0].to_far()
     units[1].to_chips()
     units[2].to_owners()
     for up in ups:
@@ -455,11 +471,13 @@
         up.relay2()
     units[3].to_owners()
     units[2].to_chips()
-    units[1].to_sibling()
+    units[1].to_far()
+    units[0].to_sibling()
     for up in ups:
         up.relay3()
     units[3].to_chips()
-    units[2].to_sibling()
+    units[2].to_far()
+    units[1].to_sibling()
     load_vcot.wait()
     own_product = cot_dot([up.own[...] for up in ups])
     own_change = own.change(own_product)
@@ -470,12 +488,14 @@
     for up in ups:
         up.settle2()
     changes.append(cot_step(1))
-    units[3].to_sibling()
+    units[3].to_far()
+    units[2].to_sibling()
     for up in ups:
         up.settle3()
     changes.append(cot_step(2))
     for up in ups:
         up.last()
+    units[3].to_sibling()
     changes.append(cot_step(3))
 
     own_mask = (label_ref[...] == me).astype(F32)
@@ -549,7 +569,7 @@
     cuts = [hidden // 128 * n // PIECES * 128 for n in range(PIECES + 1)]
     splits = [cuts[n + 1] - cuts[n] for n in range(PIECES)]
     share = rank // GROUP
-    copies = (1 + PIECES) * 28 + 3 * (GROUP - 1) + (STEPS + 1) * 2 * CHIPS
+    copies = (1 + PIECES) * 28 + 3 * (GROUP - 1) + (STEPS + 1) * (2 * CHIPS + 1)
     any_spec = pl.BlockSpec(memory_space=pl.ANY)
     vmem_spec = pl.BlockSpec(memory_space=pltpu.VMEM)
     deltas = pl.pallas_call(

time: 94.4 us -> 93 us (0.985)
  Pallas kernels: 92.4 us -> 91 us
    pallas_call x1, Pallas kernels: 92.4 us -> 91 us  [on_device(): pl.pallas_call(functools.partial(kernel, skills, reach), out_shape=jax.Sh...]
where the time goes in v5:
time: 93 us; the launch traced here: 92.8 us
  Pallas kernels  91 us (98%)
  local copies, waits for them, and re-layouts  1.25 us (1%)
    pallas_call x1, Pallas kernels, on_device(): pl.pallas_call(functools.partial(kernel, skills, reach), out_shape=jax.Sh...  91 us

profile of v5, /device:TPU:7, one launch (start us, length us, event | category | flops | bytes accessed | tf_op | source)
XLA Modules:
  0.0 92.8 jit_solution(9445240060777988275)
XLA Ops:
  0.6 91.0 %shard_map.86 = f32[2,17]{1,0:T(2,128)} custom-call(bf16[256,1024]{1,0:T(8,128)(2,1)} %bitcast.10, bf16[256,1920]{1,0:T(8,128)(2,1)} %bitcast.9, s32[1,256]{1,0:T(1,128)} %index_ref.1, bf16[512,1024]{1,0:T(8,128)(2,1)} %bitcast.8, bf16[512,1920]{1,0:T(8,128)(2,1)} %bitcast.7, s32[1,512]{1,0:T(1,128)} %label_ref.1, bf16[64,1024]{1,0:T(8,128)(2,1)} %bitcast.11), custom_call_target="tpu_custom_call" | custom-call | tf_op jit(solution)/shard_map/pallas_call | solution.py:575
  91.6 1.3 %fusion = (f32[1,17]{1,0:T(1,128)}, f32[1,17]{1,0:T(1,128)}) fusion(f32[2,17]{1,0:T(2,128)} %shard_map.86), kind=kLoop, calls=%fused_computation | loop fusion | bytes 272 | tf_op jit(solution)/shard_map/slice | solution.py:625
